TPU v7x, 32 devices: a whole 2x2x4 slice. The times are simulated.
32 devices in a mesh: wide: 8 (over y, x, core), narrow: 4 (over z).
Axes of the slice: x: 2, y: 2, z: 4, core: 2. Of those that a mesh axis runs over, the one named last changes fastest.
Arguments:
- hidden: bfloat16 [8, 256, 2048], P('wide', None, 'narrow'), may hold values from -6 to 6
- norm_gain: bfloat16 [2, 2048], replicated, may hold values from 0.25 to 1.75
- w_qkv: bfloat16 [2048, 3, 2048], P(None, None, 'narrow'), may hold values from -1 to 1
- qk_gain: float32 [2, 2048], P(None, 'narrow'), may hold values from 0.25 to 32
- w_out: bfloat16 [2048, 2048], P('narrow'), may hold values from -0.125 to 0.125
- cache: bfloat16 [2, 8, 2048, 2048], P(None, 'wide', None, 'narrow'), may hold values from -6 to 6
- lengths: int32 [8], replicated, may hold values from 1 to 2048, 8192 in all
- placing: int32 [8], replicated, may hold values from 0 to 7, each once
- routes: int32 [8, 256, 8], P('wide'), may hold values from 0 to 15, all different within a row; in each aligned block of 256 rows (0 to 255, 256 to 511, ..., all dimensions but the last counted through in order) at most 192 rows name the same one
- gate_w: float32 [8, 256, 8], P('wide'), may hold values from 0.02 to 0.3
- w_gu: bfloat16 [16, 2048, 2, 1024], P('wide', None, None, 'narrow'), may hold values from -0.125 to 0.125
- w_down: bfloat16 [16, 1024, 2048], P('wide', 'narrow'), may hold values from -0.1875 to 0.1875
Outputs:
- result: bfloat16 [8, 256, 2048], P('wide', None, 'narrow')
- new_cache: bfloat16 [2, 8, 256, 2048], P(None, 'wide', None, 'narrow')
Inputs may be any that keep to these rules, and one draw needn't show every extreme that they name: `routes`: each token names 8 different experts; among the 256 tokens of one request no expert is named more than 192 times. `lengths`: some request has 2048 cached positions. Slot s holds request placing[s]; every request is held once.
All inputs are finite; a program needn't handle non-finite values.
Results may differ from a plain program's by a relative error of at most 0.013.
Values may be sent and summed in bfloat16 or wider, within the bound.
A program may use at most 128 MiB of HBM per device.

v0:
```python
import jax
import jax.numpy as jnp
from jax import lax
from jax.sharding import PartitionSpec as P

HD = 128


def normalize(values, gain_row):
    values = values.astype(jnp.float32)
    return (
        values
        * lax.rsqrt(jnp.mean(values * values, axis=-1, keepdims=True) + 1e-05)
        * gain_row.astype(jnp.float32)
    )


def rotary(values, positions):
    half_dim = values.shape[-1] // 2
    frequency = 10000.0 ** (-(jnp.arange(half_dim, dtype=jnp.float32) * (2.0 / values.shape[-1])))
    angle = positions[:, None] * frequency[None, :]
    cosine = jnp.cos(angle)[:, None, :]
    sine_part = jnp.sin(angle)[:, None, :]
    first_half = values[..., :half_dim]
    second_half = values[..., half_dim:]
    return jnp.concatenate(
        [
            first_half * cosine - second_half * sine_part,
            second_half * cosine + first_half * sine_part,
        ],
        axis=-1,
    )


def per_device(
    hidden, norm_gain, w_qkv, qk_gain, w_out, cache, lengths, placing, routes, gate_w, w_gu, w_down
):
    narrow = lax.axis_size("narrow")
    wide_size = lax.axis_size("wide")
    column = lax.axis_index("narrow")
    position = lax.axis_index("wide")
    span_len = hidden.shape[1]
    share_cols = hidden.shape[2]
    full_width = share_cols * narrow
    tokens = lax.all_gather(hidden[0], "narrow", axis=1, tiled=True)
    normed = normalize(tokens, norm_gain[0]).astype(jnp.bfloat16)
    local_cols = w_qkv.shape[2]
    projected = jnp.dot(
        normed, w_qkv.reshape(full_width, 3 * local_cols), preferred_element_type=jnp.float32
    )
    queries = projected[:, :local_cols]
    keys_new = projected[:, local_cols : 2 * local_cols]
    values_new = projected[:, 2 * local_cols :]
    squares = lax.psum((jnp.sum(queries * queries, -1), jnp.sum(keys_new * keys_new, -1)), "narrow")
    features = local_cols * narrow
    queries = queries * lax.rsqrt(squares[0][:, None] / features + 1e-05) * qk_gain[0]
    keys_new = keys_new * lax.rsqrt(squares[1][:, None] / features + 1e-05) * qk_gain[1]
    head_count = local_cols // HD
    length = lengths[placing[position]]
    positions = length.astype(jnp.float32) + jnp.arange(span_len, dtype=jnp.float32)
    queries = rotary(queries.reshape(span_len, head_count, HD), positions).astype(jnp.bfloat16)
    keys_new = rotary(keys_new.reshape(span_len, head_count, HD), positions).astype(jnp.bfloat16)
    values_new = values_new.reshape(span_len, head_count, HD).astype(jnp.bfloat16)
    stored = cache.shape[2]
    all_keys = jnp.concatenate([cache[0, 0].reshape(stored, head_count, HD), keys_new], 0)
    all_values = jnp.concatenate([cache[1, 0].reshape(stored, head_count, HD), values_new], 0)
    scores = jnp.einsum(
        "thd,jhd->htj", queries, all_keys, preferred_element_type=jnp.float32
    ) * HD ** (-0.5)
    key_index = jnp.arange(stored + span_len, dtype=jnp.int32)[None, :]
    query_index = jnp.arange(span_len, dtype=jnp.int32)[:, None]
    allowed = jnp.where(key_index < stored, key_index < length, key_index - stored <= query_index)
    scores = jnp.where(allowed[None], scores, -1e30)
    highest = jnp.max(scores, axis=-1, keepdims=True)
    exponent = jnp.exp(scores - highest)
    weights = exponent.astype(jnp.bfloat16)
    denominator = jnp.sum(exponent, axis=-1)
    summed = jnp.einsum("htj,jhd->thd", weights, all_values, preferred_element_type=jnp.float32)
    heads_out = (
        (summed / jnp.transpose(denominator)[:, :, None])
        .astype(jnp.bfloat16)
        .reshape(span_len, local_cols)
    )
    partial_out = jnp.dot(heads_out, w_out, preferred_element_type=jnp.float32)
    attention = lax.psum(partial_out.astype(jnp.bfloat16), "narrow").astype(jnp.float32)
    after = (tokens.astype(jnp.float32) + attention).astype(jnp.bfloat16)
    after_own = lax.dynamic_slice_in_dim(after, column * share_cols, share_cols, 1)
    routed = normalize(after, norm_gain[1]).astype(jnp.bfloat16)
    chosen = routes.shape[2]
    held_experts = w_gu.shape[0]
    experts = held_experts * wide_size
    capacity = span_len * chosen * 3 // (2 * experts)
    flat_routes = routes[0].reshape(-1)
    onehot = (flat_routes[:, None] == jnp.arange(experts, dtype=jnp.int32)[None, :]).astype(
        jnp.int32
    )
    slot_rank = jnp.sum((jnp.cumsum(onehot, 0) - onehot) * onehot, 1)
    target = flat_routes * capacity + slot_rank
    token_row = jnp.arange(span_len * chosen, dtype=jnp.int32) // chosen
    source_row = jnp.full((experts * capacity,), span_len, jnp.int32).at[target].set(token_row)
    padded = jnp.concatenate([routed, jnp.zeros((1, full_width), jnp.bfloat16)], 0)
    outgoing = padded[source_row].reshape(experts, capacity, full_width)
    arrived = lax.all_to_all(outgoing, "wide", split_axis=0, concat_axis=0, tiled=True)
    inner_cols = w_gu.shape[3]
    arrived = arrived.reshape(wide_size, held_experts, capacity, full_width)
    gate_up = jnp.einsum(
        "wjcd,jdf->wjcf",
        arrived,
        w_gu.reshape(held_experts, full_width, 2 * inner_cols),
        preferred_element_type=jnp.float32,
    )
    activated = (jax.nn.silu(gate_up[..., :inner_cols]) * gate_up[..., inner_cols:]).astype(
        jnp.bfloat16
    )
    parts = jnp.einsum(
        "wjcf,jfd->wjcd", activated, w_down, preferred_element_type=jnp.float32
    ).astype(jnp.bfloat16)
    gate_scale = gate_w[0].reshape(-1)
    returned = lax.all_to_all(
        parts.reshape(experts, capacity, full_width),
        "wide",
        split_axis=0,
        concat_axis=0,
        tiled=True,
    )
    picked = returned.reshape(experts * capacity, full_width)[target].astype(jnp.float32)
    combined = jnp.sum((picked * gate_scale[:, None]).reshape(span_len, chosen, full_width), 1)
    expert_out = lax.psum_scatter(
        combined.astype(jnp.bfloat16), "narrow", scatter_dimension=1, tiled=True
    ).astype(jnp.float32)
    result = (after_own.astype(jnp.float32) + expert_out).astype(jnp.bfloat16)[None]
    fresh = jnp.stack(
        [keys_new.reshape(span_len, local_cols), values_new.reshape(span_len, local_cols)]
    )[:, None]
    return (result, fresh)


def solution(mesh):
    placed = (
        P("wide", None, "narrow"),
        P(),
        P(None, None, "narrow"),
        P(None, "narrow"),
        P("narrow", None),
        P(None, "wide", None, "narrow"),
        P(),
        P(),
        P("wide", None, None),
        P("wide", None, None),
        P("wide", None, None, "narrow"),
        P("wide", "narrow", None),
    )
    return jax.shard_map(
        per_device,
        mesh=mesh,
        in_specs=placed,
        out_specs=(P("wide", None, "narrow"), P(None, "wide", None, "narrow")),
        check_vma=False,
    )
```

profile of v0, /device:TPU:0, one launch (start us, length us, event | category | flops | bytes accessed | tf_op | source)
XLA Modules:
  0.0 548.3 jit_solution(7301213833029315441)
XLA Ops:
  7.2 0.7 all-gather.3.cloned.1.call-update
  8.0 1.2 dynamic_slice.9
  11.2 1.2 dynamic_slice.10
  13.1 0.7 iota_compare_fusion.3
  13.7 0.8 copy.33
  14.6 0.7 broadcast_multiply_fusion
  15.3 8.9 %copy.24 = bf16[2048,3,512]{0,2,1:T(8,128)(2,1)} copy(bf16[2048,3,512]{2,0,1:T(8,128)(2,1)} %param.14) | data formatting | bytes 12582912 | tf_op args[2]
  24.2 4.5 fusion.74
  28.7 4.0 copy.45
  32.7 4.0 copy.31
  36.7 4.0 copy.23
  40.8 4.5 reduce-window.6
  46.8 1.5 fusion.27
  48.3 5.0 fusion.39
  53.4 1.0 copy-done.2
  54.5 0.7 slice.97
  55.2 13.6 %all-reduce.1 = (f32[256]{0:T(256)S(1)}, f32[256]{0:T(256)S(1)}) all-reduce(f32[256]{0:T(256)S(1)} %get-tuple-element.7, f32[256]{0:T(256)S(1)} %get-tuple-element.6), channel_id=1, replica_groups=mesh['wide'=8,'narrow'=4] {'narrow'}, use_global_device_ids=true, to_apply=%region_4.0 | all-reduce | flops 512 | bytes 4096 | tf_op jit(solution)/shard_map/psum | solution.py:54
  68.9 2.3 multiply_multiply_fusion.1
  71.2 1.2 reshape.249
  72.4 1.3 fusion.75
  73.7 1.2 reshape.250
  74.9 1.2 fusion.76
  76.1 1.1 copy.42
  77.2 1.5 subtract_convert_fusion
  78.7 1.3 multiply_subtract_fusion
  80.2 2.3 fusion.3
  82.6 2.5 fusion.4
  85.1 2.6 fusion.49
  87.7 1.8 convolution_convert_fusion
  90.3 8.1 %scatter_custom_fusion = s32[3072]{0:T(1024)S(1)} fusion(s32[2048]{0:T(1024)S(1)} %bitcast.90, s32[2048]{0:T(1024)S(1)} %add_select_fusion, s32[]{:T(128)} %constant.66.clone.1), kind=kCustom, calls=%fused_computation.92 | custom fusion | bytes 12292 | tf_op jit(solution)/shard_map/scatter | solution.py:100
  98.4 41.4 %all-reduce.4.cloned.1.call-done = bf16[256,2048]{1,0:T(8,128)(2,1)} async-done(((bf16[256,2048]{1,0:T(8,128)(2,1)}), bf16[256,2048]{1,0:T(8,128)(2,1)}) %all-reduce.4.cloned.1.call-update) | async-done | bytes 1048592 | tf_op jit(solution)/shard_map/psum | solution.py:85
  139.8 1.7 fusion.24
  141.5 1.0 copy-done.1
  142.9 16.0 %gather_fusion = bf16[3072,2048]{1,0:T(8,128)(2,1)} fusion(bf16[257,2048]{1,0:T(8,128)(2,1)S(1)} %concatenate.20, s32[3072]{0:T(1024)S(1)} %fusion.62), kind=kCustom, calls=%fused_computation | custom fusion | bytes 25178112 | tf_op jit(solution)/shard_map/gather | solution.py:102
  158.9 5.6 %all-to-all-start = ((bf16[16,192,2048]{2,1,0:T(8,128)(2,1)}), bf16[16,192,2048]{2,1,0:T(8,128)(2,1)}, u32[]{:S(2)}, u32[]{:S(2)}) async-start(bf16[16,192,2048]{2,1,0:T(8,128)(2,1)} %bitcast.81), calls=%async_computation | async-start | bytes 25165824 | tf_op jit(solution)/shard_map/all_to_all | solution.py:103
  164.5 7.7 %reshape.288 = bf16[2,2048,512,1]{2,1,0,3:T(8,128)(2,1)} reshape(bf16[2,2048,2,256]{3,2,1,0:T(2,128)(2,1)} %param.22) | data formatting | bytes 8388608 | tf_op jit(solution)/shard_map/reshape | solution.py:109
  172.1 131.1 %all-to-all-done = bf16[16,192,2048]{2,1,0:T(8,128)(2,1)} async-done(((bf16[16,192,2048]{2,1,0:T(8,128)(2,1)}), bf16[16,192,2048]{2,1,0:T(8,128)(2,1)}, u32[]{:S(2)}, u32[]{:S(2)}) %all-to-all-start) | async-done | bytes 12582944 | tf_op jit(solution)/shard_map/all_to_all | solution.py:103
  303.3 12.5 %fusion.11 = f32[8,2,192,512]{3,2,0,1:T(8,128)} fusion(bf16[2,2048,512,1]{2,1,0,3:T(8,128)(2,1)} %reshape.288, bf16[8,2,192,2048]{3,2,1,0:T(8,128)(2,1)} %bitcast.19), kind=kOutput, calls=%fused_computation.21 | convolution fusion | flops 6442450944 | bytes 23068672 | tf_op jit(solution)/shard_map/wjcd,jdf->wjcf/dot_general | solution.py:106
  315.8 9.3 %convert_bitcast_fusion = bf16[8,2,192,2048]{3,2,0,1:T(8,128)(2,1)} fusion(bf16[2,256,2048]{2,1,0:T(8,128)(2,1)S(1)} %copy-done, f32[8,2,192,512]{3,2,0,1:T(8,128)} %fusion.11), kind=kOutput, calls=%fused_computation.7 | convolution fusion | flops 3232235520 | bytes 20971520 | tf_op jit(solution)/shard_map/wjcf,jfd->wjcd/dot_general | solution.py:115
  325.0 10.7 %copy.36 = bf16[8,2,192,2048]{3,2,1,0:T(8,128)(2,1)} copy(bf16[8,2,192,2048]{3,2,0,1:T(8,128)(2,1)} %convert_bitcast_fusion) | data formatting | bytes 25165824 | tf_op jit(solution)/shard_map/convert_element_type | solution.py:117
  335.8 5.5 all-to-all-start.1
  341.5 138.8 %all-to-all-done.1 = bf16[16,192,2048]{2,1,0:T(8,128)(2,1)} async-done(((bf16[16,192,2048]{2,1,0:T(8,128)(2,1)}), bf16[16,192,2048]{2,1,0:T(8,128)(2,1)}, u32[]{:S(2)}, u32[]{:S(2)}) %all-to-all-start.1) | async-done | bytes 12582944 | tf_op jit(solution)/shard_map/all_to_all | solution.py:119
  480.3 22.5 %gather_fusion.1 = bf16[2048,2048]{1,0:T(8,128)(2,1)} fusion(bf16[3072,2048]{1,0:T(8,128)(2,1)} %bitcast.26, s32[2048]{0:T(1024)S(1)} %broadcast_clamp_fusion), kind=kCustom, calls=%fused_computation.1 | custom fusion | bytes 16785408 | tf_op jit(solution)/shard_map/gather | solution.py:126
  502.8 12.2 %fusion = bf16[256,2048]{1,0:T(8,128)(2,1)} fusion(bf16[2048,2048]{1,0:T(8,128)(2,1)} %gather_fusion.1, f32[256,8]{1,0:T(8,128)S(1)} %copy.37), kind=kLoop, calls=%fused_computation.4 | loop fusion | flops 12058624 | bytes 9445376 | tf_op jit(solution)/shard_map/reduce_sum | solution.py:127
  515.4 1.1 slice_bitcast_fusion
  516.5 0.8 maximum_bitcast_fusion
  517.3 22.6 %reduce-scatter.2.cloned.1.call-done = bf16[256,512]{1,0:T(8,128)(2,1)} async-done(((bf16[256,2048]{1,0:T(8,128)(2,1)}), bf16[256,512]{1,0:T(8,128)(2,1)}) %reduce-scatter.2.cloned.1.call-update) | async-done | bytes 262160 | tf_op jit(solution)/shard_map/reduce_scatter | solution.py:128
  539.9 1.8 fusion.54
  (66 shorter events, 3.6 us)
Async XLA Ops:
  7.2 308.6 %copy-start = (bf16[2,256,2048]{2,1,0:T(8,128)(2,1)S(1)}, bf16[2,256,2048]{2,1,0:T(8,128)(2,1)}, u32[]{:S(2)}) copy-start(bf16[2,256,2048]{2,1,0:T(8,128)(2,1)} %param.23) | copy-start | bytes 6291460
  7.2 39.6 %all-gather.3.cloned.1.call-start = ((), (), s32[]{:S(2)}) async-start(), calls=%async_computation.5 | async-start | bytes 1310720 | tf_op jit(solution)/shard_map/all_gather | solution.py:45
  7.9 131.8 %all-reduce.4.cloned.1.call-start = ((), (), s32[]{:S(2)}) async-start(), calls=%async_computation.3 | async-start | bytes 2097152 | tf_op jit(solution)/shard_map/psum | solution.py:85
  14.6 26.1 %copy-start.7 = (s32[1,256,8]{2,1,0:T(8,128)}, s32[1,256,8]{2,1,0:T(8,128)S(1)}, u32[]{:S(2)}) copy-start(s32[1,256,8]{2,1,0:T(8,128)S(1)} %copy.33) | copy-start | bytes 24580
  32.7 13.1 %copy-start.15 = (f32[2,512]{1,0:T(2,128)S(1)}, f32[2,512]{1,0:T(2,128)}, u32[]{:S(2)}) copy-start(f32[2,512]{1,0:T(2,128)} %param.15) | copy-start | bytes 12292
  32.7 13.6 %copy-start.13 = (bf16[2,2048]{1,0:T(2,128)(2,1)S(1)}, bf16[2,2048]{1,0:T(2,128)(2,1)}, u32[]{:S(2)}) copy-start(bf16[2,2048]{1,0:T(2,128)(2,1)} %param.13) | copy-start | bytes 24580
  45.3 8.0 %copy-start.9 = (s32[16,16,128]{2,1,0:T(8,128)}, s32[16,16,128]{2,1,0:T(8,128)S(1)}, u32[]{:S(2)}) copy-start(s32[16,16,128]{2,1,0:T(8,128)S(1)} %reduce-window.6) | copy-start | bytes 393220
  53.3 1.2 copy-start.2
  77.2 3.0 copy-start.5
  80.2 2.3 copy-start.11
  82.5 2.5 copy-start.4
  85.1 2.7 copy-start.6
  87.7 1.8 copy-start.8
  87.7 2.4 copy-start.10
  87.7 52.0 %copy-start.3 = (bf16[1,256,2048]{2,1,0:T(8,128)(2,1)S(1)}, bf16[1,256,2048]{2,1,0:T(8,128)(2,1)}, u32[]{:S(2)}) copy-start(bf16[1,256,2048]{2,1,0:T(8,128)(2,1)} %all-gather.3.cloned.1.call-done) | copy-start | bytes 3145732
  141.5 1.0 copy-start.1
  158.9 144.4 %all-to-all-start = ((bf16[16,192,2048]{2,1,0:T(8,128)(2,1)}), bf16[16,192,2048]{2,1,0:T(8,128)(2,1)}, u32[]{:S(2)}, u32[]{:S(2)}) async-start(bf16[16,192,2048]{2,1,0:T(8,128)(2,1)} %bitcast.81), calls=%async_computation | async-start | bytes 25165824 | tf_op jit(solution)/shard_map/all_to_all | solution.py:103
  335.8 5.5 %copy-start.14 = (f32[1,256,8]{1,2,0:T(8,128)S(1)}, f32[1,256,8]{1,2,0:T(8,128)}, u32[]{:S(2)}) copy-start(f32[1,256,8]{1,2,0:T(8,128)} %param.21) | copy-start | bytes 24580
  335.8 144.5 %all-to-all-start.1 = ((bf16[16,192,2048]{2,1,0:T(8,128)(2,1)}), bf16[16,192,2048]{2,1,0:T(8,128)(2,1)}, u32[]{:S(2)}, u32[]{:S(2)}) async-start(bf16[16,192,2048]{2,1,0:T(8,128)(2,1)} %bitcast.80), calls=%async_computation.1 | async-start | bytes 25165824 | tf_op jit(solution)/shard_map/all_to_all | solution.py:119
  341.3 198.7 %reduce-scatter.2.cloned.1.call-start = ((), (), s32[]{:S(2)}) async-start(), calls=%async_computation.4 | async-start | bytes 1310720 | tf_op jit(solution)/shard_map/reduce_scatter | solution.py:128
  502.8 12.3 %copy-start.12 = (bf16[256,4,128]{2,0,1:T(8,128)(2,1)S(1)}, bf16[256,4,128]{2,0,1:T(8,128)(2,1)}, u32[]{:S(2)}) copy-start(bf16[256,4,128]{2,0,1:T(8,128)(2,1)} %copy-done.11) | copy-start | bytes 786436
Sparse Core Ops, SparseCore 0:
  9.6 30.6 all-gather.2
  89.7 50.0 all-reduce.3
  515.2 24.7 reduce-scatter.1
where the time goes:
time: 550 us; the launch traced here: 548 us
  waiting for transfers between devices  335 us (61%)
  local copies, waits for them, and re-layouts  105 us (19%)
  other arithmetic  33.7 us (6%)
  matrix products  33.4 us (6%)
  between operations  16.8 us (3%)
  blocking collectives  13.6 us (2%)
  starting transfers between devices  11.2 us (2%)
    all_to_all x1, waiting for transfers between devices, per_device(): lax.all_to_all(parts.reshape(experts, capacity, full_width), 'wide', spli...  139 us
    all_to_all x1, waiting for transfers between devices, per_device(): lax.all_to_all(outgoing, 'wide', split_axis=0, concat_axis=0, tiled=True)  131 us
    psum x1, waiting for transfers between devices, per_device(): lax.psum(partial_out.astype(jnp.bfloat16), 'narrow').astype(jnp.float32)  41.4 us
    reduce_scatter x1, waiting for transfers between devices, per_device(): lax.psum_scatter(combined.astype(jnp.bfloat16), 'narrow', scatter_dimensi...  22.6 us
    gather x1, local copies, waits for them, and re-layouts, per_device(): returned.reshape(experts * capacity, full_width)[target].astype(jnp.float32)  22.5 us
    gather x1, local copies, waits for them, and re-layouts, per_device(): outgoing = padded[source_row].reshape(experts, capacity, full_width)  16 us
    unnamed x35, local copies, waits for them, and re-layouts  15.7 us
    psum x1, blocking collectives, per_device(): lax.psum((jnp.sum(queries * queries, -1), jnp.sum(keys_new * keys_new, -1...  13.6 us
  transfers between devices with their start and end apart: 5, of which 4 were waited for; matrix products, arithmetic and copies ran while one was open for 10% of the time, Pallas kernels for 0%

commit v1 on v0

--- a/solution.py
+++ b/solution.py
@@ -82,51 +82,42 @@
         .reshape(span_len, local_cols)
     )
     partial_out = jnp.dot(heads_out, w_out, preferred_element_type=jnp.float32)
-    attention = lax.psum(partial_out.astype(jnp.bfloat16), "narrow").astype(jnp.float32)
-    after = (tokens.astype(jnp.float32) + attention).astype(jnp.bfloat16)
-    after_own = lax.dynamic_slice_in_dim(after, column * share_cols, share_cols, 1)
-    routed = normalize(after, norm_gain[1]).astype(jnp.bfloat16)
-    chosen = routes.shape[2]
+    rows = span_len // narrow
+    attention = lax.psum_scatter(
+        partial_out.astype(jnp.bfloat16), "narrow", scatter_dimension=0, tiled=True
+    ).astype(jnp.float32)
+    own_rows = lax.dynamic_slice_in_dim(tokens, column * rows, rows, 0)
+    after_rows = (own_rows.astype(jnp.float32) + attention).astype(jnp.bfloat16)
+    after_all = lax.all_gather(after_rows, ("wide", "narrow"), axis=0, tiled=True)
+    after_own = lax.dynamic_slice(
+        after_all, (position * span_len, column * share_cols), (span_len, share_cols)
+    )
+    routed = normalize(after_all, norm_gain[1]).astype(jnp.bfloat16)
     held_experts = w_gu.shape[0]
+    inner_cols = w_gu.shape[3]
     experts = held_experts * wide_size
-    capacity = span_len * chosen * 3 // (2 * experts)
-    flat_routes = routes[0].reshape(-1)
-    onehot = (flat_routes[:, None] == jnp.arange(experts, dtype=jnp.int32)[None, :]).astype(
-        jnp.int32
-    )
-    slot_rank = jnp.sum((jnp.cumsum(onehot, 0) - onehot) * onehot, 1)
-    target = flat_routes * capacity + slot_rank
-    token_row = jnp.arange(span_len * chosen, dtype=jnp.int32) // chosen
-    source_row = jnp.full((experts * capacity,), span_len, jnp.int32).at[target].set(token_row)
-    padded = jnp.concatenate([routed, jnp.zeros((1, full_width), jnp.bfloat16)], 0)
-    outgoing = padded[source_row].reshape(experts, capacity, full_width)
-    arrived = lax.all_to_all(outgoing, "wide", split_axis=0, concat_axis=0, tiled=True)
-    inner_cols = w_gu.shape[3]
-    arrived = arrived.reshape(wide_size, held_experts, capacity, full_width)
-    gate_up = jnp.einsum(
-        "wjcd,jdf->wjcf",
-        arrived,
-        w_gu.reshape(held_experts, full_width, 2 * inner_cols),
+    named = routes[0][:, :, None] == jnp.arange(experts, dtype=jnp.int32)[None, None, :]
+    table = jnp.sum(jnp.where(named, gate_w[0][:, :, None], 0.0), axis=1)
+    table = lax.all_gather(table, "wide", axis=0, tiled=True)
+    scale = lax.dynamic_slice_in_dim(table, position * held_experts, held_experts, 1)
+    pieces = []
+    for j in range(held_experts):
+        gate_up = jnp.dot(
+            routed,
+            w_gu[j].reshape(full_width, 2 * inner_cols),
+            preferred_element_type=jnp.float32,
+        )
+        activated = jax.nn.silu(gate_up[:, :inner_cols]) * gate_up[:, inner_cols:]
+        pieces.append((activated * scale[:, j : j + 1]).astype(jnp.bfloat16))
+    weighted = jnp.concatenate(pieces, 1)
+    combined = jnp.dot(
+        weighted,
+        w_down.reshape(held_experts * inner_cols, full_width),
         preferred_element_type=jnp.float32,
-    )
-    activated = (jax.nn.silu(gate_up[..., :inner_cols]) * gate_up[..., inner_cols:]).astype(
-        jnp.bfloat16
-    )
-    parts = jnp.einsum(
-        "wjcf,jfd->wjcd", activated, w_down, preferred_element_type=jnp.float32
     ).astype(jnp.bfloat16)
-    gate_scale = gate_w[0].reshape(-1)
-    returned = lax.all_to_all(
-        parts.reshape(experts, capacity, full_width),
-        "wide",
-        split_axis=0,
-        concat_axis=0,
-        tiled=True,
-    )
-    picked = returned.reshape(experts * capacity, full_width)[target].astype(jnp.float32)
-    combined = jnp.sum((picked * gate_scale[:, None]).reshape(span_len, chosen, full_width), 1)
+    combined = lax.psum_scatter(combined, "wide", scatter_dimension=0, tiled=True)
     expert_out = lax.psum_scatter(
-        combined.astype(jnp.bfloat16), "narrow", scatter_dimension=1, tiled=True
+        combined, "narrow", scatter_dimension=1, tiled=True
     ).astype(jnp.float32)
     result = (after_own.astype(jnp.float32) + expert_out).astype(jnp.bfloat16)[None]
     fresh = jnp.stack(

time: 550 us -> 325 us (0.59)
  waiting for transfers between devices: 335 us -> 181 us
  local copies, waits for them, and re-layouts: 105 us -> 50.2 us
  other arithmetic: 33.7 us -> 22 us
  starting transfers between devices: 11.2 us -> 0.2 us
  blocking collectives: 13.6 us -> 22.9 us
    all_to_all x2 -> x0, waiting for transfers between devices: 270 us -> none  [the longest x1 139 us: per_device(): lax.all_to_all(parts.reshape(experts, capacity, full_width), 'wide', spli...]
    reduce_scatter x1 -> x3, waiting for transfers between devices: 22.6 us -> 123 us  [the longest x1 70 us: per_device(): lax.psum_scatter(combined, 'wide', scatter_dimension=0, tiled=True)]
    all_gather x0 -> x1, waiting for transfers between devices: none -> 57.8 us  [per_device(): lax.all_gather(after_rows, ('wide', 'narrow'), axis=0, tiled=True)]
    psum x1 -> x0, waiting for transfers between devices: 41.4 us -> none  [per_device(): lax.psum(partial_out.astype(jnp.bfloat16), 'narrow').astype(jnp.float32)]
    gather x2 -> x0, local copies, waits for them, and re-layouts: 38.5 us -> none  [the longest x1 22.5 us: per_device(): returned.reshape(experts * capacity, full_width)[target].astype(jnp.float32)]
    reduce_sum x2 -> x1, other arithmetic: 12.3 us -> 0.02 us  [per_device(): table = jnp.sum(jnp.where(named, gate_w[0][:, :, None], 0.0), axis=1)]
    all_to_all x2 -> x0, starting transfers between devices: 11 us -> none  [the longest x1 5.56 us: per_device(): lax.all_to_all(outgoing, 'wide', split_axis=0, concat_axis=0, tiled=True)]
    convert_element_type x1 -> x0, local copies, waits for them, and re-layouts: 10.7 us -> none  [per_device(): parts = jnp.einsum('wjcf,jfd->wjcd', activated, w_down, preferred_element...]
  transfers between devices with their start and end apart: 5 -> 5, of which waited for: 4 -> 5; matrix products, arithmetic and copies ran while one was open for 10% -> 13% of each run, Pallas kernels for 0% -> 0%
where the time goes in v1:
time: 325 us; the launch traced here: 324 us
  waiting for transfers between devices  181 us (56%)
  local copies, waits for them, and re-layouts  50.2 us (15%)
  matrix products  30.7 us (9%)
  blocking collectives  22.9 us (7%)
  other arithmetic  22 us (7%)
  between operations  16.6 us (5%)
    reduce_scatter x1, waiting for transfers between devices, per_device(): lax.psum_scatter(combined, 'wide', scatter_dimension=0, tiled=True)  70 us
    all_gather x1, waiting for transfers between devices, per_device(): lax.all_gather(after_rows, ('wide', 'narrow'), axis=0, tiled=True)  57.8 us
    reduce_scatter x1, waiting for transfers between devices, per_device(): lax.psum_scatter(combined, 'narrow', scatter_dimension=1, tiled=True)  27 us
    reduce_scatter x1, waiting for transfers between devices, per_device(): lax.psum_scatter(partial_out.astype(jnp.bfloat16), 'narrow', scatter_dime...  25.5 us
    unnamed x30, local copies, waits for them, and re-layouts  20.6 us
    psum x1, blocking collectives, per_device(): lax.psum((jnp.sum(queries * queries, -1), jnp.sum(keys_new * keys_new, -1...  13.5 us
    dot_general x2, matrix products, per_device(): jnp.dot(routed, w_gu[j].reshape(full_width, 2 * inner_cols), preferred_el...  12.3 us
    all_gather x1, blocking collectives, per_device(): table = lax.all_gather(table, 'wide', axis=0, tiled=True)  9.38 us
  transfers between devices with their start and end apart: 5, of which 5 were waited for; matrix products, arithmetic and copies ran while one was open for 13% of the time, Pallas kernels for 0%

profile of v1, /device:TPU:0, one launch (start us, length us, event | category | flops | bytes accessed | tf_op | source)
XLA Modules:
  0.0 323.8 jit_solution(17968152327370127640)
XLA Ops:
  7.2 0.7 all-gather.6.cloned.1.call-update
  8.0 1.2 dynamic_slice.16
  11.2 1.2 dynamic_slice.17
  13.1 0.7 iota_compare_fusion.2
  13.7 8.8 %copy.38 = bf16[2048,3,512]{0,2,1:T(8,128)(2,1)} copy(bf16[2048,3,512]{2,0,1:T(8,128)(2,1)} %param.14) | data formatting | bytes 12582912 | tf_op args[2]
  22.6 4.5 %fusion.62 = (bf16[1,1,2048,512]{3,2,1,0:T(8,128)(2,1)}, bf16[1,1,2048,512]{3,2,1,0:T(8,128)(2,1)}) fusion(bf16[2,1,2048,512]{3,2,1,0:T(8,128)(2,1)} %param.17), kind=kLoop, calls=%fused_computation.87 | loop fusion | bytes 8388608 | tf_op jit(solution)/shard_map/slice | solution.py:66
  27.1 4.0 %copy.51 = bf16[1,1,2048,512]{2,3,1,0:T(8,128)(2,1)} copy(bf16[1,1,2048,512]{3,2,1,0:T(8,128)(2,1)} %get-tuple-element.15) | data formatting | bytes 4194304
  31.1 4.0 %copy.45 = bf16[2048,4,128]{2,0,1:T(8,128)(2,1)} copy(bf16[2048,4,128]{0,2,1:T(8,128)(2,1)} %bitcast.54) | data formatting | bytes 4194304 | tf_op jit(solution)/shard_map/reshape;squeeze | solution.py:65
  35.1 4.0 %copy.37 = bf16[1,1,2048,512]{2,3,1,0:T(8,128)(2,1)} copy(bf16[1,1,2048,512]{3,2,1,0:T(8,128)(2,1)} %get-tuple-element.14) | data formatting | bytes 4194304 | tf_op jit(solution)/shard_map/slice | solution.py:66
  39.1 0.5 multiply_cosine_fusion
  39.7 0.4 fusion.20
  40.2 1.5 fusion.21
  41.8 5.0 %fusion.36 = f32[256,1536]{1,0:T(8,128)S(1)} fusion(bf16[2048,1536]{0,1:T(8,128)(2,1)} %bitcast.57, bf16[1,256,2048]{2,1,0:T(8,128)(2,1)} %all-gather.6.cloned.1.call-done, f32[2048]{0:T(1024)S(1)} %bitcast.71, f32[256]{0:T(256)S(1)} %add_rsqrt_fusion.3), kind=kOutput, calls=%fused_computation.40 | convolution fusion | flops 1612709888 | bytes 8922112 | tf_op jit(solution)/shard_map/dot_general | solution.py:48
  46.9 1.0 copy-done.2
  47.9 0.7 slice.114
  48.6 13.5 %all-reduce = (f32[256]{0:T(256)S(1)}, f32[256]{0:T(256)S(1)}) all-reduce(f32[256]{0:T(256)S(1)} %get-tuple-element.9, f32[256]{0:T(256)S(1)} %get-tuple-element.8), channel_id=1, replica_groups=mesh['wide'=8,'narrow'=4] {'narrow'}, use_global_device_ids=true, to_apply=%region_4.0 | all-reduce | flops 512 | bytes 4096 | tf_op jit(solution)/shard_map/psum | solution.py:54
  62.1 2.3 multiply_multiply_fusion.1
  64.4 1.2 reshape.184
  65.7 1.3 fusion.63
  66.9 1.2 reshape.185
  68.1 1.3 fusion.64
  69.4 1.8 copy.48
  71.2 1.5 subtract_convert_fusion
  72.7 1.2 multiply_subtract_fusion
  74.1 2.3 fusion.3
  76.4 2.5 fusion.4
  79.0 2.6 fusion.46
  81.6 1.7 convolution_convert_fusion.1
  83.4 25.5 %reduce-scatter.4.cloned.1.call-done = bf16[64,2048]{1,0:T(8,128)(2,1)} async-done(((bf16[256,2048]{1,0:T(8,128)(2,1)}), bf16[64,2048]{1,0:T(8,128)(2,1)}) %reduce-scatter.4.cloned.1.call-update) | async-done | bytes 262160 | tf_op jit(solution)/shard_map/reduce_scatter | solution.py:86
  108.9 1.8 fusion.51
  110.7 5.7 %fusion.61 = (bf16[1,2048,2,256]{3,2,1,0:T(2,128)(2,1)S(1)}, bf16[1,2048,2,256]{3,2,1,0:T(2,128)(2,1)}) fusion(bf16[2,2048,2,256]{3,2,1,0:T(2,128)(2,1)} %param.22), kind=kLoop, calls=%fused_computation.86 | loop fusion | bytes 8388608 | tf_op jit(solution)/shard_map/slice | solution.py:107
  116.4 1.8 copy.54
  118.2 3.5 %copy.55 = bf16[256,8,2,256]{3,1,2,0:T(8,128)(2,1)} copy(bf16[256,8,2,256]{3,2,1,0:T(2,128)(2,1)} %bitcast.55) | data formatting | bytes 4194304
  121.7 9.4 %all_gather.11 = f32[2048,16]{0,1:T(8,128)S(1)} all-gather(f32[256,16]{0,1:T(8,128)S(1)} %select_reduce_fusion), channel_id=1, replica_groups=mesh['wide'=8,'narrow'=4] {'wide'}, dimensions={0}, use_global_device_ids=true | all-gather | bytes 147456 | tf_op jit(solution)/shard_map/all_gather | solution.py:101
  131.1 57.8 %all-gather.4.cloned.1.call-done = bf16[2048,2048]{1,0:T(8,128)(2,1)} async-done(((bf16[64,2048]{1,0:T(8,128)(2,1)}), bf16[2048,2048]{1,0:T(8,128)(2,1)}) %all-gather.4.cloned.1.call-update) | async-done | bytes 8388624 | tf_op jit(solution)/shard_map/all_gather | solution.py:91
  189.0 5.2 %fusion = f32[2048]{0:T(1024)S(1)} fusion(bf16[2048,2048]{1,0:T(8,128)(2,1)} %all-gather.4.cloned.1.call-done), kind=kLoop, calls=%fused_computation.2 | loop fusion | flops 12580864 | bytes 8396800 | tf_op jit(solution)/shard_map/reduce_sum | solution.py:13
  194.2 0.5 copy-done.1
  194.7 6.8 %fusion.11 = f32[2048,512]{0,1:T(8,128)S(1)} fusion(bf16[2048,512]{1,0:T(8,128)(2,1)} %bitcast.59, bf16[2048,2048]{1,0:T(8,128)(2,1)S(1)} %copy-done.1, f32[2048]{0:T(1024)S(1)} %bitcast.69, f32[2048]{0:T(1024)S(1)} %add_rsqrt_fusion), kind=kOutput, calls=%fused_computation.17 | convolution fusion | flops 4311744512 | bytes 14696448 | tf_op jit(solution)/shard_map/dot_general | solution.py:105
  201.6 0.7 fusion.27
  202.2 0.9 copy-done.5
  203.2 5.5 %fusion.9 = f32[2048,512]{0,1:T(8,128)S(1)} fusion(bf16[2048,512]{1,0:T(8,128)(2,1)S(1)} %bitcast.60, bf16[2048,2048]{1,0:T(8,128)(2,1)S(1)} %copy-done.1, f32[2048]{0:T(1024)S(1)} %bitcast.70, f32[2048]{0:T(1024)S(1)} %add_rsqrt_fusion), kind=kOutput, calls=%fused_computation.16 | convolution fusion | flops 4311744512 | bytes 14696448 | tf_op jit(solution)/shard_map/dot_general | solution.py:105
  208.7 0.7 fusion.25
  209.3 6.7 %convolution_convert_fusion = bf16[2048,2048]{1,0:T(8,128)(2,1)} fusion(bf16[512,2048]{1,0:T(8,128)(2,1)S(1)} %bitcast.53, bf16[2048,256]{0,1:T(8,128)(2,1)S(1)} %fusion.25, bf16[2048,256]{0,1:T(8,128)(2,1)S(1)} %fusion.27), kind=kOutput, calls=%fused_computation.8 | convolution fusion | flops 4303355904 | bytes 12582912 | tf_op jit(solution)/shard_map/dot_general | solution.py:113
  216.2 70.0 %reduce-scatter.6.cloned.1.call-done = bf16[256,2048]{1,0:T(8,128)(2,1)} async-done(((bf16[2048,2048]{1,0:T(8,128)(2,1)}), bf16[256,2048]{1,0:T(8,128)(2,1)}) %reduce-scatter.6.cloned.1.call-update) | async-done | bytes 1048592 | tf_op jit(solution)/shard_map/reduce_scatter | solution.py:118
  286.5 1.1 slice_bitcast_fusion
  287.6 0.8 maximum_bitcast_fusion
  288.4 27.0 %reduce-scatter.8.cloned.1.call-done = bf16[256,512]{1,0:T(8,128)(2,1)} async-done(((bf16[256,2048]{1,0:T(8,128)(2,1)}), bf16[256,512]{1,0:T(8,128)(2,1)}) %reduce-scatter.8.cloned.1.call-update) | async-done | bytes 262160 | tf_op jit(solution)/shard_map/reduce_scatter | solution.py:119
  315.5 1.8 fusion.52
  (47 shorter events, 1.2 us)
Async XLA Ops:
  7.2 202.2 %copy-start = (bf16[2,256,2048]{2,1,0:T(8,128)(2,1)S(1)}, bf16[2,256,2048]{2,1,0:T(8,128)(2,1)}, u32[]{:S(2)}) copy-start(bf16[2,256,2048]{2,1,0:T(8,128)(2,1)} %param.23) | copy-start | bytes 6291460
  7.2 33.1 %all-gather.6.cloned.1.call-start = ((), (), s32[]{:S(2)}) async-start(), calls=%async_computation.7 | async-start | bytes 1310720 | tf_op jit(solution)/shard_map/all_gather | solution.py:45
  7.9 101.0 %reduce-scatter.4.cloned.1.call-start = ((), (), s32[]{:S(2)}) async-start(), calls=%async_computation.3 | async-start | bytes 1310720 | tf_op jit(solution)/shard_map/reduce_scatter | solution.py:86
  35.1 4.0 %copy-start.12 = (f32[2,512]{1,0:T(2,128)S(1)}, f32[2,512]{1,0:T(2,128)}, u32[]{:S(2)}) copy-start(f32[2,512]{1,0:T(2,128)} %param.15) | copy-start | bytes 12292
  35.1 4.5 %copy-start.9 = (bf16[2,2048]{1,0:T(2,128)(2,1)S(1)}, bf16[2,2048]{1,0:T(2,128)(2,1)}, u32[]{:S(2)}) copy-start(bf16[2,2048]{1,0:T(2,128)(2,1)} %param.13) | copy-start | bytes 24580
  46.7 1.2 copy-start.2
  69.4 3.3 %copy-start.6 = (f32[256,4,64]{2,1,0:T(4,128)S(1)}, f32[256,4,64]{2,1,0:T(4,128)}, u32[]{:S(2)}) copy-start(f32[256,4,64]{2,1,0:T(4,128)} %get-tuple-element.24) | copy-start | bytes 786436
  71.2 2.8 copy-start.4
  76.4 2.5 copy-start.3
  76.4 2.5 copy-start.8
  79.0 2.6 copy-start.7
  83.3 105.6 %all-gather.4.cloned.1.call-start = ((), (), s32[]{:S(2)}) async-start(), calls=%async_computation.4 | async-start | bytes 8650752 | tf_op jit(solution)/shard_map/all_gather | solution.py:91
  110.7 175.5 %reduce-scatter.6.cloned.1.call-start = ((), (), s32[]{:S(2)}) async-start(), calls=%async_computation.5 | async-start | bytes 9437184 | tf_op jit(solution)/shard_map/reduce_scatter | solution.py:118
  118.2 3.5 %copy-start.10 = (f32[1,256,8]{1,2,0:T(8,128)S(1)}, f32[1,256,8]{1,2,0:T(8,128)}, u32[]{:S(2)}) copy-start(f32[1,256,8]{1,2,0:T(8,128)} %param.21) | copy-start | bytes 24580
  118.2 3.5 %copy-start.11 = (s32[1,256,8]{1,2,0:T(8,128)S(1)}, s32[1,256,8]{1,2,0:T(8,128)}, u32[]{:S(2)}) copy-start(s32[1,256,8]{1,2,0:T(8,128)} %param.20) | copy-start | bytes 24580
  189.0 5.8 %copy-start.1 = (bf16[2048,2048]{1,0:T(8,128)(2,1)S(1)}, bf16[2048,2048]{1,0:T(8,128)(2,1)}, u32[]{:S(2)}) copy-start(bf16[2048,2048]{1,0:T(8,128)(2,1)} %all-gather.4.cloned.1.call-done) | copy-start | bytes 25165828
  201.6 1.6 copy-start.5
  216.1 99.4 %reduce-scatter.8.cloned.1.call-start = ((), (), s32[]{:S(2)}) async-start(), calls=%async_computation.6 | async-start | bytes 1310720 | tf_op jit(solution)/shard_map/reduce_scatter | solution.py:119
Sparse Core Ops, SparseCore 0:
  9.6 30.6 all-gather.5
  83.5 25.3 reduce-scatter.3
  112.8 76.1 all-gather.3
  216.2 69.8 reduce-scatter.5
  288.3 27.1 reduce-scatter.7

commit v2 on v1

--- a/solution.py
+++ b/solution.py
@@ -1,6 +1,8 @@
 import jax
 import jax.numpy as jnp
 from jax import lax
+from jax.experimental import pallas as pl
+from jax.experimental.pallas import tpu as pltpu
 from jax.sharding import PartitionSpec as P
 
 HD = 128
@@ -31,6 +33,373 @@
         axis=-1,
     )
 
+
+TAIL = 128
+VMEM_LIMIT = 56 * 1024 * 1024
+
+
+def places():
+    w = lax.axis_index("wide")
+    z = lax.axis_index("narrow")
+    c = lax.rem(w, 2)
+    dx = 2 - 4 * lax.rem(lax.div(w, 2), 2)
+    dy = 4 - 8 * lax.div(w, 4)
+    first = dx * (1 - c) + dy * c
+    second = dy * (1 - c) + dx * c
+    return w, z, 1 - 2 * c, first, second
+
+
+def greet(w, z, sib, first, second):
+    barrier = pltpu.get_barrier_semaphore()
+    for step in (sib, first, second):
+        pl.semaphore_signal(
+            barrier, inc=1, device_id={"wide": w + step}, device_id_type=pl.DeviceIdType.MESH
+        )
+    for k in (1, 2, 3):
+        pl.semaphore_signal(
+            barrier,
+            inc=1,
+            device_id={"narrow": lax.rem(z + k, 4)},
+            device_id_type=pl.DeviceIdType.MESH,
+        )
+    pl.semaphore_wait(barrier, 6)
+
+
+def gather_kernel(rows_ref, gu_ref, out_ref, held, send, recv):
+    w, z, sib, first, second = places()
+    width = gu_ref.shape[1]
+    inner = gu_ref.shape[2] // 2
+    experts_held = gu_ref.shape[0]
+    experts = experts_held * 8
+    mine = (0, first, second, first + second)
+    theirs = (sib, sib + second, sib + first, sib + first + second)
+    slots = [w + step for step in mine + theirs]
+    held[z, w] = rows_ref[...]
+    greet(w, z, sib, first, second)
+    started = []
+
+    def piece(slot, k, role, device):
+        ref = held.at[lax.rem(z + 4 - k, 4), slot]
+        return pltpu.make_async_remote_copy(
+            src_ref=ref,
+            dst_ref=ref,
+            send_sem=send.at[len(started)],
+            recv_sem=recv.at[role, k],
+            device_id=device,
+            device_id_type=pl.DeviceIdType.MESH,
+        )
+
+    def push(slot, k, role, step):
+        copy = piece(slot, k, role, {"wide": w + step})
+        copy.start()
+        started.append(copy)
+
+    def arrive(role, k):
+        ref = held.at[lax.rem(z + 4 - k, 4), slots[role]]
+        pltpu.make_async_remote_copy(
+            src_ref=ref,
+            dst_ref=ref,
+            send_sem=send.at[0],
+            recv_sem=recv.at[role, k],
+            device_id={"wide": w + sib},
+            device_id_type=pl.DeviceIdType.MESH,
+        ).wait_recv()
+
+    def expert_rows(k):
+        group = lax.rem(z + 4 - k, 4)
+
+        def half(h, carry):
+            rows = held.shape[2]
+            values = held[group, pl.ds(h * 4, 4)]
+            inputs = values[:, :, :width].reshape(4 * rows, width)
+            tail = values[:, :, width:].reshape(4 * rows, TAIL).astype(jnp.float32)
+            lane = lax.broadcasted_iota(jnp.int32, tail.shape, 1)
+            for j in range(experts_held):
+                e = w * experts_held + j
+                hit = (lane == e) | (lane == e + experts) | (lane == e + 2 * experts)
+                scale = jnp.sum(jnp.where(hit, tail, 0.0), axis=1, keepdims=True)
+                both = jnp.dot(inputs, gu_ref[j], preferred_element_type=jnp.float32)
+                gate = both[:, :inner]
+                active = gate / (1.0 + jnp.exp(-gate)) * both[:, inner:] * scale
+                out_ref[group, pl.ds(h * 4, 4), :, j * inner : (j + 1) * inner] = active.astype(
+                    jnp.bfloat16
+                ).reshape(4, rows, inner)
+            return carry
+
+        lax.fori_loop(0, 2, half, 0)
+
+    for k in (1, 3, 2):
+        ref = held.at[z, w]
+        copy = pltpu.make_async_remote_copy(
+            src_ref=ref,
+            dst_ref=ref,
+            send_sem=send.at[len(started)],
+            recv_sem=recv.at[0, k],
+            device_id={"narrow": lax.rem(z + k, 4)},
+            device_id_type=pl.DeviceIdType.MESH,
+        )
+        copy.start()
+        started.append(copy)
+    order = (0, 1, 3, 2)
+    for t in range(7):
+        if t < 4:
+            k = order[t]
+            if k:
+                arrive(0, k)
+            push(w, k, 1, first)
+            push(w, k, 2, second)
+            push(w, k, 4, sib)
+        if 1 <= t < 5:
+            k = order[t - 1]
+            arrive(1, k)
+            push(slots[1], k, 3, second)
+            push(slots[1], k, 5, sib)
+            arrive(2, k)
+            push(slots[2], k, 6, sib)
+        if 2 <= t < 6:
+            k = order[t - 2]
+            arrive(3, k)
+            push(slots[3], k, 7, sib)
+        if 3 <= t:
+            k = order[t - 3]
+            for role in (4, 5, 6, 7):
+                arrive(role, k)
+            expert_rows(k)
+    for copy in started:
+        copy.wait_send()
+
+
+def gather_experts(rows_in, gu):
+    rows, padded = rows_in.shape
+    held, _, both = gu.shape
+    return pl.pallas_call(
+        gather_kernel,
+        out_shape=jax.ShapeDtypeStruct((4, 8, rows, held * both // 2), jnp.bfloat16),
+        in_specs=[pl.BlockSpec(memory_space=pltpu.VMEM)] * 2,
+        out_specs=pl.BlockSpec(memory_space=pltpu.VMEM),
+        scratch_shapes=[
+            pltpu.VMEM((4, 8, rows, padded), jnp.bfloat16),
+            pltpu.SemaphoreType.DMA((31,)),
+            pltpu.SemaphoreType.DMA((8, 4)),
+        ],
+        compiler_params=pltpu.CompilerParams(
+            collective_id=0, has_side_effects=True, vmem_limit_bytes=VMEM_LIMIT
+        ),
+        name="gather_experts",
+    )(rows_in, gu)
+
+
+def reduce_kernel(
+    weighted_ref,
+    down_ref,
+    after_ref,
+    out_ref,
+    sib_out,
+    sib_in,
+    first_out,
+    first_keep,
+    first_in,
+    second_out,
+    second_keep,
+    second_in,
+    z_out,
+    z_in,
+    after_in,
+    total,
+    send,
+    recv,
+):
+    w, z, sib, first, second = places()
+    span, cols = out_ref.shape
+    rows = after_ref.shape[0]
+    mine = (0, first, second, first + second)
+    theirs = (sib, sib + second, sib + first, sib + first + second)
+    greet(w, z, sib, first, second)
+    started = []
+
+    def push(src, dst, number, device):
+        copy = pltpu.make_async_remote_copy(
+            src_ref=src,
+            dst_ref=dst,
+            send_sem=send.at[number],
+            recv_sem=recv.at[number],
+            device_id=device,
+            device_id_type=pl.DeviceIdType.MESH,
+        )
+        copy.start()
+        started.append(copy)
+
+    def arrive(dst, number):
+        pltpu.make_async_remote_copy(
+            src_ref=dst,
+            dst_ref=dst,
+            send_sem=send.at[number],
+            recv_sem=recv.at[number],
+            device_id={"wide": w + sib},
+            device_id_type=pl.DeviceIdType.MESH,
+        ).wait_recv()
+
+    def columns(k):
+        return pl.ds(pl.multiple_of(lax.rem(z + k, 4) * cols, cols), cols)
+
+    def product(slot, k):
+        values = weighted_ref[:, slot].reshape(span, weighted_ref.shape[3])
+        return jnp.dot(values, down_ref[:, columns(k)], preferred_element_type=jnp.float32)
+
+    for k in (1, 3, 2):
+        push(
+            after_ref.at[:, columns(k)],
+            after_in.at[k],
+            20 + k,
+            {"narrow": lax.rem(z + k, 4)},
+        )
+    order = (2, 1, 3, 0)
+    for t in range(7):
+        if t < 4:
+            k = order[t]
+            for r in range(4):
+                sib_out[k, r] = product(w + theirs[r], k).astype(jnp.bfloat16)
+            push(sib_out.at[k], sib_in.at[k], k, {"wide": w + sib})
+        if 1 <= t < 5:
+            k = order[t - 1]
+            arrive(sib_in.at[k], k)
+            for spot, r in ((0, 1), (1, 3)):
+                value = product(w + mine[r], k) + sib_in[k, r].astype(jnp.float32)
+                first_out[k, spot] = value.astype(jnp.bfloat16)
+            push(first_out.at[k], first_in.at[k], 4 + k, {"wide": w + first})
+            for spot, r in ((0, 0), (1, 2)):
+                first_keep[k, spot] = product(w + mine[r], k) + sib_in[k, r].astype(jnp.float32)
+        if 2 <= t < 6:
+            k = order[t - 2]
+            arrive(first_in.at[k], 4 + k)
+            second_out[k] = (first_keep[k, 1] + first_in[k, 1].astype(jnp.float32)).astype(
+                jnp.bfloat16
+            )
+            push(second_out.at[k], second_in.at[k], 8 + k, {"wide": w + second})
+            second_keep[k] = first_keep[k, 0] + first_in[k, 0].astype(jnp.float32)
+        if 3 <= t:
+            k = order[t - 3]
+            arrive(second_in.at[k], 8 + k)
+            value = second_keep[k] + second_in[k].astype(jnp.float32)
+            if k:
+                z_out[k] = value.astype(jnp.bfloat16)
+                push(z_out.at[k], z_in.at[k], 12 + k, {"narrow": lax.rem(z + k, 4)})
+            else:
+                total[...] = value
+    for k in (1, 2, 3):
+        arrive(z_in.at[k], 12 + k)
+        arrive(after_in.at[k], 20 + k)
+    total[...] = total[...] + (
+        z_in[1].astype(jnp.float32) + z_in[2].astype(jnp.float32) + z_in[3].astype(jnp.float32)
+    )
+    for k in range(4):
+        block = pl.ds(pl.multiple_of(lax.rem(z + 4 - k, 4) * rows, rows), rows)
+        own = after_in[k] if k else after_ref[:, columns(0)]
+        out_ref[block, :] = (total[block, :] + own.astype(jnp.float32)).astype(jnp.bfloat16)
+    for copy in started:
+        copy.wait_send()
+
+
+def reduce_experts(weighted, down, after_rows):
+    rows, width = after_rows.shape
+    span, cols = rows * 4, width // 4
+    half = jnp.bfloat16
+    return pl.pallas_call(
+        reduce_kernel,
+        out_shape=jax.ShapeDtypeStruct((span, cols), half),
+        in_specs=[pl.BlockSpec(memory_space=pltpu.VMEM)] * 3,
+        out_specs=pl.BlockSpec(memory_space=pltpu.VMEM),
+        scratch_shapes=[
+            pltpu.VMEM((4, 4, span, cols), half),
+            pltpu.VMEM((4, 4, span, cols), half),
+            pltpu.VMEM((4, 2, span, cols), half),
+            pltpu.VMEM((4, 2, span, cols), jnp.float32),
+            pltpu.VMEM((4, 2, span, cols), half),
+            pltpu.VMEM((4, span, cols), half),
+            pltpu.VMEM((4, span, cols), jnp.float32),
+            pltpu.VMEM((4, span, cols), half),
+            pltpu.VMEM((4, span, cols), half),
+            pltpu.VMEM((4, span, cols), half),
+            pltpu.VMEM((4, rows, cols), half),
+            pltpu.VMEM((span, cols), jnp.float32),
+            pltpu.SemaphoreType.DMA((24,)),
+            pltpu.SemaphoreType.DMA((24,)),
+        ],
+        compiler_params=pltpu.CompilerParams(
+            collective_id=1, has_side_effects=True, vmem_limit_bytes=VMEM_LIMIT
+        ),
+        name="reduce_experts",
+    )(weighted, down, after_rows)
+
+
+def router_table(routes, gate_w, experts):
+    named = routes[:, :, None] == jnp.arange(experts, dtype=jnp.int32)[None, None, :]
+    return jnp.sum(jnp.where(named, gate_w[:, :, None], 0.0), axis=1)
+
+
+def in_three(values):
+    high = values.astype(jnp.bfloat16)
+    rest = values - high.astype(jnp.float32)
+    middle = rest.astype(jnp.bfloat16)
+    low = (rest - middle.astype(jnp.float32)).astype(jnp.bfloat16)
+    return [high, middle, low]
+
+
+def experts_by_copies(after_rows, gain, routes, gate_w, w_gu, w_down):
+    rows, width = after_rows.shape
+    held, _, _, inner = w_gu.shape
+    experts = held * 8
+    column = lax.axis_index("narrow")
+    routed = normalize(after_rows, gain).astype(jnp.bfloat16)
+    table = router_table(
+        lax.dynamic_slice_in_dim(routes, column * rows, rows, 0),
+        lax.dynamic_slice_in_dim(gate_w, column * rows, rows, 0),
+        experts,
+    )
+    filler = jnp.zeros((rows, TAIL - 3 * experts), jnp.bfloat16)
+    rows_in = jnp.concatenate([routed] + in_three(table) + [filler], 1)
+    weighted = gather_experts(rows_in, w_gu.reshape(held, width, 2 * inner))
+    return reduce_experts(weighted, w_down.reshape(held * inner, width), after_rows)
+
+
+def experts_by_collectives(after_rows, gain, routes, gate_w, w_gu, w_down):
+    position = lax.axis_index("wide")
+    column = lax.axis_index("narrow")
+    wide_size = lax.axis_size("wide")
+    narrow = lax.axis_size("narrow")
+    rows, full_width = after_rows.shape
+    span_len, share_cols = rows * narrow, full_width // narrow
+    after_all = lax.all_gather(after_rows, ("wide", "narrow"), axis=0, tiled=True)
+    after_own = lax.dynamic_slice(
+        after_all, (position * span_len, column * share_cols), (span_len, share_cols)
+    )
+    routed = normalize(after_all, gain).astype(jnp.bfloat16)
+    held_experts = w_gu.shape[0]
+    inner_cols = w_gu.shape[3]
+    experts = held_experts * wide_size
+    table = router_table(routes, gate_w, experts)
+    table = lax.all_gather(table, "wide", axis=0, tiled=True)
+    scale = lax.dynamic_slice_in_dim(table, position * held_experts, held_experts, 1)
+    pieces = []
+    for j in range(held_experts):
+        gate_up = jnp.dot(
+            routed,
+            w_gu[j].reshape(full_width, 2 * inner_cols),
+            preferred_element_type=jnp.float32,
+        )
+        activated = jax.nn.silu(gate_up[:, :inner_cols]) * gate_up[:, inner_cols:]
+        pieces.append((activated * scale[:, j : j + 1]).astype(jnp.bfloat16))
+    weighted = jnp.concatenate(pieces, 1)
+    combined = jnp.dot(
+        weighted,
+        w_down.reshape(held_experts * inner_cols, full_width),
+        preferred_element_type=jnp.float32,
+    ).astype(jnp.bfloat16)
+    combined = lax.psum_scatter(combined, "wide", scatter_dimension=0, tiled=True)
+    expert_out = lax.psum_scatter(
+        combined, "narrow", scatter_dimension=1, tiled=True
+    ).astype(jnp.float32)
+    return (after_own.astype(jnp.float32) + expert_out).astype(jnp.bfloat16)
 
 def per_device(
     hidden, norm_gain, w_qkv, qk_gain, w_out, cache, lengths, placing, routes, gate_w, w_gu, w_down
@@ -88,38 +457,9 @@
     ).astype(jnp.float32)
     own_rows = lax.dynamic_slice_in_dim(tokens, column * rows, rows, 0)
     after_rows = (own_rows.astype(jnp.float32) + attention).astype(jnp.bfloat16)
-    after_all = lax.all_gather(after_rows, ("wide", "narrow"), axis=0, tiled=True)
-    after_own = lax.dynamic_slice(
-        after_all, (position * span_len, column * share_cols), (span_len, share_cols)
-    )
-    routed = normalize(after_all, norm_gain[1]).astype(jnp.bfloat16)
-    held_experts = w_gu.shape[0]
-    inner_cols = w_gu.shape[3]
-    experts = held_experts * wide_size
-    named = routes[0][:, :, None] == jnp.arange(experts, dtype=jnp.int32)[None, None, :]
-    table = jnp.sum(jnp.where(named, gate_w[0][:, :, None], 0.0), axis=1)
-    table = lax.all_gather(table, "wide", axis=0, tiled=True)
-    scale = lax.dynamic_slice_in_dim(table, position * held_experts, held_experts, 1)
-    pieces = []
-    for j in range(held_experts):
-        gate_up = jnp.dot(
-            routed,
-            w_gu[j].reshape(full_width, 2 * inner_cols),
-            preferred_element_type=jnp.float32,
-        )
-        activated = jax.nn.silu(gate_up[:, :inner_cols]) * gate_up[:, inner_cols:]
-        pieces.append((activated * scale[:, j : j + 1]).astype(jnp.bfloat16))
-    weighted = jnp.concatenate(pieces, 1)
-    combined = jnp.dot(
-        weighted,
-        w_down.reshape(held_experts * inner_cols, full_width),
-        preferred_element_type=jnp.float32,
-    ).astype(jnp.bfloat16)
-    combined = lax.psum_scatter(combined, "wide", scatter_dimension=0, tiled=True)
-    expert_out = lax.psum_scatter(
-        combined, "narrow", scatter_dimension=1, tiled=True
-    ).astype(jnp.float32)
-    result = (after_own.astype(jnp.float32) + expert_out).astype(jnp.bfloat16)[None]
+    by_copies = wide_size == 8 and narrow == 4 and w_gu.shape[0] * 24 <= TAIL
+    experts_of = experts_by_copies if by_copies else experts_by_collectives
+    result = experts_of(after_rows, norm_gain[1], routes[0], gate_w[0], w_gu, w_down)[None]
     fresh = jnp.stack(
         [keys_new.reshape(span_len, local_cols), values_new.reshape(span_len, local_cols)]
     )[:, None]

time: 325 us -> 226 us (0.70)
  waiting for transfers between devices: 181 us -> 16.1 us
  Pallas kernels: 0 us -> 105 us
  matrix products: 30.7 us -> 11.6 us
  blocking collectives: 22.9 us -> 13.4 us
  other arithmetic: 22 us -> 13.2 us
    pallas_call x0 -> x2, Pallas kernels: none -> 105 us  [the longest x1 53.5 us: reduce_experts(): pl.pallas_call(reduce_kernel, out_shape=jax.ShapeDtypeStruct((span, cols)...]
    reduce_scatter x2 -> x0, waiting for transfers between devices: 97 us -> none  [the longest x1 70 us: per_device(): lax.psum_scatter(combined, 'wide', scatter_dimension=0, tiled=True)]
    all_gather x1 -> x0, waiting for transfers between devices: 57.8 us -> none  [per_device(): lax.all_gather(after_rows, ('wide', 'narrow'), axis=0, tiled=True)]
    dot_general x3 -> x0, matrix products: 19.1 us -> none  [the longest x2 12.3 us: per_device(): jnp.dot(routed, w_gu[j].reshape(full_width, 2 * inner_cols), preferred_el...]
    reduce_scatter x1, waiting for transfers between devices: 25.5 us -> 15.3 us  [per_device(): lax.psum_scatter(partial_out.astype(jnp.bfloat16), 'narrow', scatter_dime...]
    all_gather x1 -> x0, blocking collectives: 9.38 us -> none  [per_device(): table = lax.all_gather(table, 'wide', axis=0, tiled=True)]
    reshape x0 -> x1, local copies, waits for them, and re-layouts: none -> 7.61 us  [experts_by_copies(): weighted = gather_experts(rows_in, w_gu.reshape(held, width, 2 * inner))]
    slice x2 -> x0, local copies, waits for them, and re-layouts: 5.68 us -> none  [the longest x1 5.66 us: per_device(): w_gu[j].reshape(full_width, 2 * inner_cols)]
  transfers between devices with their start and end apart: 5 -> 2, of which waited for: 5 -> 2; matrix products, arithmetic and copies ran while one was open for 13% -> 18% of each run, Pallas kernels for 0% -> 0%
where the time goes in v2:
time: 226 us; the launch traced here: 225 us
  Pallas kernels  105 us (46%)
  local copies, waits for them, and re-layouts  48.2 us (21%)
  between operations  16.9 us (7%)
  waiting for transfers between devices  16.1 us (7%)
  blocking collectives  13.4 us (6%)
  other arithmetic  13.2 us (6%)
  matrix products  11.6 us (5%)
    pallas_call x1, Pallas kernels, reduce_experts(): pl.pallas_call(reduce_kernel, out_shape=jax.ShapeDtypeStruct((span, cols)...  53.5 us
    pallas_call x1, Pallas kernels, gather_experts(): pl.pallas_call(gather_kernel, out_shape=jax.ShapeDtypeStruct((4, 8, rows,...  51.5 us
    unnamed x25, local copies, waits for them, and re-layouts  15.6 us
    reduce_scatter x1, waiting for transfers between devices, per_device(): lax.psum_scatter(partial_out.astype(jnp.bfloat16), 'narrow', scatter_dime...  15.3 us
    psum x1, blocking collectives, per_device(): lax.psum((jnp.sum(queries * queries, -1), jnp.sum(keys_new * keys_new, -1...  13.4 us
    slice x2, local copies, waits for them, and re-layouts, per_device(): cache[1, 0].reshape(stored, head_count, HD)  8.51 us
    reshape x1, local copies, waits for them, and re-layouts, experts_by_copies(): weighted = gather_experts(rows_in, w_gu.reshape(held, width, 2 * inner))  7.61 us
    dot_general x1, matrix products, per_device(): jnp.dot(normed, w_qkv.reshape(full_width, 3 * local_cols), preferred_elem...  4.96 us
  transfers between devices with their start and end apart: 2, of which 2 were waited for; matrix products, arithmetic and copies ran while one was open for 18% of the time, Pallas kernels for 0%

profile of v2, /device:TPU:0, one launch (start us, length us, event | category | flops | bytes accessed | tf_op | source)
XLA Modules:
  0.0 224.6 jit_solution(18268435001089232554)
XLA Ops:
  7.2 0.7 all-gather.3.cloned.1.call-update
  7.9 0.0 reduce-scatter.2.cloned.1.call-start
  8.0 1.2 dynamic_slice.16
  11.2 1.2 dynamic_slice.17
  13.1 0.7 iota_compare_fusion.2
  13.7 8.9 %copy.49 = bf16[2048,3,512]{0,2,1:T(8,128)(2,1)} copy(bf16[2048,3,512]{2,0,1:T(8,128)(2,1)} %param.14) | data formatting | bytes 12582912 | tf_op args[2]
  22.6 4.5 %fusion.50 = (bf16[1,1,2048,512]{3,2,1,0:T(8,128)(2,1)}, bf16[1,1,2048,512]{3,2,1,0:T(8,128)(2,1)}) fusion(bf16[2,1,2048,512]{3,2,1,0:T(8,128)(2,1)} %param.17), kind=kLoop, calls=%fused_computation.74 | loop fusion | bytes 8388608 | tf_op jit(solution)/shard_map/slice | solution.py:435
  27.2 4.0 %copy.65 = bf16[1,1,2048,512]{2,3,1,0:T(8,128)(2,1)} copy(bf16[1,1,2048,512]{3,2,1,0:T(8,128)(2,1)} %get-tuple-element.17) | data formatting | bytes 4194304
  31.1 4.0 %copy.56 = bf16[2048,4,128]{2,0,1:T(8,128)(2,1)} copy(bf16[2048,4,128]{0,2,1:T(8,128)(2,1)} %bitcast.44) | data formatting | bytes 4194304 | tf_op jit(solution)/shard_map/reshape;squeeze | solution.py:434
  35.1 4.0 %copy.48 = bf16[1,1,2048,512]{2,3,1,0:T(8,128)(2,1)} copy(bf16[1,1,2048,512]{3,2,1,0:T(8,128)(2,1)} %get-tuple-element.16) | data formatting | bytes 4194304 | tf_op jit(solution)/shard_map/slice | solution.py:435
  39.1 0.5 multiply_cosine_fusion
  39.6 0.4 fusion.13
  40.1 0.2 all-gather.3.cloned.1.call-done
  40.2 1.5 fusion.14
  41.8 5.0 %fusion.22 = f32[256,1536]{1,0:T(8,128)S(1)} fusion(bf16[2048,1536]{0,1:T(8,128)(2,1)} %bitcast.45, bf16[1,256,2048]{2,1,0:T(8,128)(2,1)} %all-gather.3.cloned.1.call-done, f32[2048]{0:T(1024)S(1)} %bitcast.54, f32[256]{0:T(256)S(1)} %add_rsqrt_fusion.2), kind=kOutput, calls=%fused_computation.23 | convolution fusion | flops 1612709888 | bytes 8922112 | tf_op jit(solution)/shard_map/dot_general | solution.py:417
  46.7 0.2 multiply_reduce_fusion.1
  46.9 1.0 copy-done.1
  47.9 0.7 slice.66
  48.7 13.4 %all-reduce = (f32[256]{0:T(256)S(1)}, f32[256]{0:T(256)S(1)}) all-reduce(f32[256]{0:T(256)S(1)} %get-tuple-element.11, f32[256]{0:T(256)S(1)} %get-tuple-element.10), channel_id=1, replica_groups=mesh['wide'=8,'narrow'=4] {'narrow'}, use_global_device_ids=true, to_apply=%region_4.0 | all-reduce | flops 512 | bytes 4096 | tf_op jit(solution)/shard_map/psum | solution.py:423
  62.1 2.3 %multiply_multiply_fusion.1 = (f32[256,512]{1,0:T(8,128)}, f32[256,512]{1,0:T(8,128)}) fusion(f32[256,1536]{1,0:T(8,128)} %copy-done.1, f32[512]{0:T(512)S(1)} %bitcast.52, f32[256]{0:T(256)S(1)} %get-tuple-element.41, f32[512]{0:T(512)S(1)} %bitcast.53, f32[256]{0:T(256)S(1)} %get-tuple-element.40), kind=kLoop, calls=%fused_computation.45 | loop fusion | flops 524288 | bytes 2103296 | tf_op jit(solution)/shard_map/mul | solution.py:425
  64.4 1.2 reshape.191
  65.6 1.3 fusion.51
  66.9 1.2 reshape.192
  68.2 1.2 fusion.52
  69.4 1.9 copy.62
  71.3 1.5 subtract_convert_fusion
  72.8 1.2 multiply_subtract_fusion
  74.0 0.1 maximum_convert_fusion
  74.1 2.3 %fusion = (f32[4,256]{1,0:T(4,128)S(1)}, f32[4,256,2304]{2,1,0:T(8,128)S(1)}) fusion(pred[256,2304]{1,0:T(8,128)(4,1)S(1)} %fusion.13, bf16[256,4,128]{2,0,1:T(8,128)(2,1)S(1)} %maximum_convert_fusion, bf16[2048,4,128]{2,0,1:T(8,128)(2,1)S(1)} %copy-done.4, bf16[256,4,64]{2,0,1:T(8,128)(2,1)S(1)} %get-tuple-element.21, ...), kind=kOutput, calls=%fused_computation.2 | convolution fusion | flops 616299520 | bytes 12652544 | tf_op jit(solution)/shard_map/thd,jhd->htj/dot_general | solution.py:436
  76.4 2.5 %fusion.1 = f32[4,256]{1,0:T(4,128)S(1)} fusion(f32[4,256,2304]{2,1,0:T(8,128)S(1)} %get-tuple-element.37, f32[4,256]{1,0:T(4,128)S(1)} %get-tuple-element.36, pred[256,2304]{1,0:T(8,128)(4,1)S(1)} %fusion.13), kind=kLoop, calls=%fused_computation.3 | loop fusion | flops 9436160 | bytes 10035200 | tf_op jit(solution)/shard_map/reduce_sum | solution.py:446
  79.0 2.6 %fusion.32 = bf16[256,4,128]{0,2,1:T(8,128)(2,1)S(1)} fusion(f32[4,256,2304]{2,1,0:T(8,128)S(1)} %get-tuple-element.37, f32[4,256]{1,0:T(4,128)S(1)} %get-tuple-element.36, pred[256,2304]{1,0:T(8,128)(4,1)S(1)} %fusion.13, bf16[256,4,128]{0,2,1:T(8,128)(2,1)S(1)} %bitcast.49, bf16[2048,4,128]{0,2,1:T(8,128)(2,1)S(1)} %bitcast.47, f32[256,4]{0,1:T(4,128)S(1)} %bitcast.55), kind=kOutput, calls=%fused_computation.28 | convolution fusion | flops 618397696 | bytes 12656640 | tf_op jit(solution)/shard_map/htj,jhd->thd/dot_general | solution.py:447
  81.6 1.7 convolution_convert_fusion
  83.4 0.1 dynamic-slice_bitcast_fusion
  83.5 0.1 dynamic-slice_bitcast_fusion.1
  83.6 0.1 copy.58
  83.7 0.1 copy.59
  83.8 7.6 %reshape.194.gu_ref = bf16[2,2048,512]{2,1,0:T(8,128)(2,1)} reshape(bf16[2,2048,2,256]{3,2,1,0:T(2,128)(2,1)} %param.22) | data formatting | bytes 8388608 | tf_op jit(solution)/shard_map/reshape | solution.py:361
  91.4 0.2 copy.60
  91.6 0.1 convert_element_type.95
  91.7 1.1 slice_bitcast_fusion
  92.8 0.8 maximum_bitcast_fusion
  93.6 15.3 %reduce-scatter.2.cloned.1.call-done = bf16[64,2048]{1,0:T(8,128)(2,1)} async-done(((bf16[256,2048]{1,0:T(8,128)(2,1)}), bf16[64,2048]{1,0:T(8,128)(2,1)}) %reduce-scatter.2.cloned.1.call-update) | async-done | bytes 262160 | tf_op jit(solution)/shard_map/reduce_scatter | solution.py:455
  108.9 1.2 fusion.37
  110.1 0.1 fusion.39
  110.3 0.8 concatenate.20.rows_ref
  111.1 51.5 %gather_experts.1.weighted_ref = bf16[4,8,64,512]{3,2,1,0:T(8,128)(2,1)} custom-call(bf16[64,2176]{1,0:T(8,128)(2,1)} %concatenate.20.rows_ref, bf16[2,2048,512]{2,1,0:T(8,128)(2,1)} %reshape.194.gu_ref), custom_call_target="tpu_custom_call" | custom-call | tf_op jit(solution)/shard_map/gather_experts/pallas_call | solution.py:175
  162.6 53.5 %reduce_experts.1 = bf16[256,512]{1,0:T(8,128)(2,1)} custom-call(bf16[4,8,64,512]{3,2,1,0:T(8,128)(2,1)} %gather_experts.1.weighted_ref, bf16[512,2048]{1,0:T(8,128)(2,1)} %bitcast.46, bf16[64,2048]{1,0:T(8,128)(2,1)} %copy-done.2), custom_call_target="tpu_custom_call" | custom-call | tf_op jit(solution)/shard_map/reduce_experts/pallas_call | solution.py:307
  216.1 1.7 copy.77
  (35 shorter events, 0.2 us)
Async XLA Ops:
  7.2 74.5 %copy-start = (bf16[512,2048]{1,0:T(8,128)(2,1)S(1)}, bf16[512,2048]{1,0:T(8,128)(2,1)}, u32[]{:S(2)}) copy-start(bf16[512,2048]{1,0:T(8,128)(2,1)} %param.16) | copy-start | bytes 6291460
  7.2 33.1 %all-gather.3.cloned.1.call-start = ((), (), s32[]{:S(2)}) async-start(), calls=%async_computation.2 | async-start | bytes 1310720 | tf_op jit(solution)/shard_map/all_gather | solution.py:414
  7.9 101.0 %reduce-scatter.2.cloned.1.call-start = ((), (), s32[]{:S(2)}) async-start(), calls=%async_computation.1 | async-start | bytes 1310720 | tf_op jit(solution)/shard_map/reduce_scatter | solution.py:455
  35.1 4.0 %copy-start.8 = (f32[2,512]{1,0:T(2,128)S(1)}, f32[2,512]{1,0:T(2,128)}, u32[]{:S(2)}) copy-start(f32[2,512]{1,0:T(2,128)} %param.15) | copy-start | bytes 12292
  35.1 4.5 %copy-start.7 = (bf16[2,2048]{1,0:T(2,128)(2,1)S(1)}, bf16[2,2048]{1,0:T(2,128)(2,1)}, u32[]{:S(2)}) copy-start(bf16[2,2048]{1,0:T(2,128)(2,1)} %param.13) | copy-start | bytes 24580
  46.7 1.2 copy-start.1
  69.4 3.4 %copy-start.5 = (f32[256,4,64]{2,1,0:T(4,128)S(1)}, f32[256,4,64]{2,1,0:T(4,128)}, u32[]{:S(2)}) copy-start(f32[256,4,64]{2,1,0:T(4,128)} %get-tuple-element.26) | copy-start | bytes 786436
  71.3 2.8 %copy-start.4 = (bf16[2048,4,128]{2,0,1:T(8,128)(2,1)S(1)}, bf16[2048,4,128]{2,0,1:T(8,128)(2,1)}, u32[]{:S(2)}) copy-start(bf16[2048,4,128]{2,0,1:T(8,128)(2,1)} %copy.56) | copy-start | bytes 6291460
  76.4 2.5 %copy-start.3 = (bf16[1,1,2048,512]{2,3,1,0:T(8,128)(2,1)S(1)}, bf16[1,1,2048,512]{2,3,1,0:T(8,128)(2,1)}, u32[]{:S(2)}) copy-start(bf16[1,1,2048,512]{2,3,1,0:T(8,128)(2,1)} %copy.48) | copy-start | bytes 6291460
  76.4 2.5 %copy-start.6 = (bf16[256,512]{0,1:T(8,128)(2,1)S(1)}, bf16[256,512]{0,1:T(8,128)(2,1)}, u32[]{:S(2)}) copy-start(bf16[256,512]{0,1:T(8,128)(2,1)} %copy.62) | copy-start | bytes 786436
  81.6 1.8 copy-start.9
  81.6 1.9 copy-start.10
  110.1 52.5 %copy-start.2 = (bf16[64,2048]{1,0:T(8,128)(2,1)}, bf16[64,2048]{1,0:T(8,128)(2,1)S(1)}, u32[]{:S(2)}) copy-start(bf16[64,2048]{1,0:T(8,128)(2,1)S(1)} %get-tuple-element.15.after_ref) | copy-start | bytes 786436
Sparse Core Ops, SparseCore 0:
  9.6 30.6 all-gather.2
  83.5 25.3 reduce-scatter.1

commit v3 on v2

--- a/solution.py
+++ b/solution.py
@@ -345,21 +345,345 @@
     return [high, middle, low]
 
 
-def experts_by_copies(after_rows, gain, routes, gate_w, w_gu, w_down):
-    rows, width = after_rows.shape
+def attend_kernel(
+    length_ref,
+    hidden_ref,
+    gain_ref,
+    qk_gain_ref,
+    cosine_ref,
+    sine_ref,
+    tail_ref,
+    w_qkv_any,
+    cache_any,
+    w_out_any,
+    rows_ref,
+    after_ref,
+    fresh_ref,
+    pieces,
+    w_qkv,
+    cache,
+    w_out,
+    projected,
+    squares,
+    heads,
+    product,
+    right_out,
+    right_in,
+    left_out,
+    left_in,
+    loads,
+    send,
+    recv,
+    stat_send_ref,
+    stat_sems,
+    stat_in_ref,
+    stat_in_sems,
+    sum_send,
+    sum_recv,
+):
+    z = lax.axis_index("narrow")
+    span, cols = hidden_ref.shape
+    rows, width = after_ref.shape
+    copies = [
+        pltpu.make_async_copy(w_qkv_any, w_qkv, loads.at[0]),
+        pltpu.make_async_copy(cache_any, cache, loads.at[1]),
+        pltpu.make_async_copy(w_out_any, w_out, loads.at[2]),
+    ]
+    for copy in copies:
+        copy.start()
+    barrier = pltpu.get_barrier_semaphore()
+    for k in (1, 2, 3):
+        pl.semaphore_signal(
+            barrier,
+            inc=1,
+            device_id={"narrow": lax.rem(z + k, 4)},
+            device_id_type=pl.DeviceIdType.MESH,
+        )
+    pieces[z] = hidden_ref[...]
+    pl.semaphore_wait(barrier, 3)
+
+    def remote(src, dst, send_sem, recv_sem, target):
+        return pltpu.make_async_remote_copy(
+            src_ref=src,
+            dst_ref=dst,
+            send_sem=send_sem,
+            recv_sem=recv_sem,
+            device_id={"narrow": target},
+            device_id_type=pl.DeviceIdType.MESH,
+        )
+
+    def hop(way, s):
+        d = (way + 1) // 2
+        spot = pieces.at[lax.rem(z - way * s + 4, 4)]
+        return remote(spot, spot, send.at[d, s], recv.at[d, s], lax.rem(z + way + 4, 4))
+
+    def can_send(way, s):
+        return (z + way >= 0) & (z + way <= 3) & (z - way * s >= 0) & (z - way * s <= 3)
+
+    def has_come(way, s):
+        return (z - way * (s + 1) >= 0) & (z - way * (s + 1) <= 3)
+
+    def arrival(way, s):
+        d = (way + 1) // 2
+        spot = pieces.at[lax.rem(z - way * (s + 1) + 4, 4)]
+        return remote(spot, spot, send.at[d, s], recv.at[d, s], lax.rem(z + 1, 4))
+
+    def begin(way, s):
+        @pl.when(can_send(way, s))
+        def _():
+            hop(way, s).start()
+
+    begin(1, 0)
+    begin(-1, 0)
+
+    def contribute(src, start):
+        values = pieces[src].astype(jnp.float32)
+        at = pl.ds(pl.multiple_of(src * cols, cols), cols)
+        scaled = (values * gain_ref[0:1, at].astype(jnp.float32)).astype(jnp.bfloat16)
+        square = jnp.sum(values * values, axis=1, keepdims=True)
+        for i in range(3):
+            term = jnp.dot(scaled, w_qkv[i, at, :], preferred_element_type=jnp.float32)
+            projected[i] = term if start else projected[i] + term
+        wide = jnp.broadcast_to(square, squares.shape)
+        squares[...] = wide if start else squares[...] + wide
+
+    copies[0].wait()
+    contribute(z, True)
+    for s in range(3):
+        for way in (1, -1):
+
+            @pl.when(has_come(way, s))
+            def _(way=way, s=s):
+                arrival(way, s).wait_recv()
+
+            if s < 2:
+                begin(way, s + 1)
+
+    def rest(k, carry):
+        contribute(lax.rem(z + k, 4), False)
+        return carry
+
+    lax.fori_loop(1, 4, rest, 0)
+    scale = lax.rsqrt(squares[:, :1] / width + 1e-05)
+    for i in range(3):
+        projected[i] = projected[i] * scale
+    lane = lax.broadcasted_iota(jnp.int32, (span, 128), 1)
+    both = [jnp.sum(projected[i] * projected[i], axis=1, keepdims=True) for i in range(2)]
+    table = jnp.where(lane == 0, both[0], jnp.where(lane == 1, both[1], 0.0))
+    stat_send_ref[...] = table.T[:8]
+    outgoing = [
+        remote(
+            stat_send_ref,
+            stat_in_ref.at[k],
+            stat_sems.at[k],
+            stat_in_sems.at[k],
+            lax.rem(z + k, 4),
+        )
+        for k in (1, 2, 3)
+    ]
+    for copy in outgoing:
+        copy.start()
+    fresh_ref[1] = projected[2].astype(jnp.bfloat16)
+    for copy in outgoing:
+        copy.wait_recv()
+    totals = stat_send_ref[...] + stat_in_ref[1] + stat_in_ref[2] + stat_in_ref[3]
+    column = jnp.concatenate([totals, jnp.zeros((120, span), jnp.float32)], 0).T
+    scales = lax.rsqrt(column / width + 1e-05)
+    for copy in outgoing:
+        copy.wait_send()
+    projected[0] = projected[0] * scales[:, 0:1] * qk_gain_ref[0:1, :]
+    projected[1] = projected[1] * scales[:, 1:2] * qk_gain_ref[1:2, :]
+    copies[1].wait()
+    length = length_ref[0]
+    stored = cache.shape[1]
+    old_allowed = lax.broadcasted_iota(jnp.int32, (1, stored), 1) < length
+    new_allowed = lax.broadcasted_iota(jnp.int32, (span, span), 1) <= lax.broadcasted_iota(
+        jnp.int32, (span, span), 0
+    )
+    across = (((1,), (1,)), ((), ()))
+
+    def head(h, carry):
+        at = pl.ds(pl.multiple_of(h * HD, HD), HD)
+        cosine, sine = cosine_ref[...], sine_ref[...]
+
+        def turned(i):
+            values = projected[i, :, at]
+            return (values * cosine + pltpu.roll(values, HD // 2, 1) * sine).astype(jnp.bfloat16)
+
+        query, key = turned(0), turned(1)
+        fresh_ref[0, :, at] = key
+        old = lax.dot_general(query, cache[0, :, at], across, preferred_element_type=jnp.float32)
+        new = lax.dot_general(query, key, across, preferred_element_type=jnp.float32)
+        old = jnp.where(old_allowed, old * HD ** (-0.5), -1e30)
+        new = jnp.where(new_allowed, new * HD ** (-0.5), -1e30)
+        highest = jnp.maximum(
+            jnp.max(old, axis=1, keepdims=True), jnp.max(new, axis=1, keepdims=True)
+        )
+        old, new = jnp.exp(old - highest), jnp.exp(new - highest)
+        denominator = jnp.sum(old, axis=1, keepdims=True) + jnp.sum(new, axis=1, keepdims=True)
+        summed = jnp.dot(
+            old.astype(jnp.bfloat16), cache[1, :, at], preferred_element_type=jnp.float32
+        ) + jnp.dot(
+            new.astype(jnp.bfloat16), fresh_ref[1, :, at], preferred_element_type=jnp.float32
+        )
+        heads[:, at] = (summed / denominator).astype(jnp.bfloat16)
+        return carry
+
+    lax.fori_loop(0, cols // HD, head, 0)
+    copies[2].wait()
+
+    def project(i, carry):
+        at = pl.ds(pl.multiple_of(i * cols, cols), cols)
+        product[:, :, at] = jnp.dot(
+            heads[...], w_out[:, at], preferred_element_type=jnp.float32
+        ).reshape(4, rows, cols)
+        return carry
+
+    lax.fori_loop(0, width // cols, project, 0)
+
+    def onward(way, d):
+        out, into = (right_out, right_in) if way > 0 else (left_out, left_in)
+        side = (way + 1) // 2
+        return remote(
+            out.at[d], into.at[d], sum_send.at[side, d], sum_recv.at[side, d], lax.rem(z + way + 4, 4)
+        )
+
+    def passing(way, d):
+        return z < d if way > 0 else z > d
+
+    for right, left in ((3, 0), (2, 1), (1, 2)):
+        for way, d in ((1, right), (-1, left)):
+            out, into = (right_out, right_in) if way > 0 else (left_out, left_in)
+            first = z == 0 if way > 0 else z == 3
+
+            @pl.when(passing(way, d) & first)
+            def _(way=way, d=d, out=out):
+                out[d] = product[d].astype(jnp.bfloat16)
+                onward(way, d).start()
+
+            @pl.when(passing(way, d) & jnp.logical_not(first))
+            def _(way=way, d=d, out=out, into=into):
+                onward(way, d).wait_recv()
+                out[d] = (product[d] + into[d].astype(jnp.float32)).astype(jnp.bfloat16)
+                onward(way, d).start()
+
+    @pl.when(z > 0)
+    def _():
+        onward(1, z).wait_recv()
+        product[z] = product[z] + right_in[z].astype(jnp.float32)
+
+    @pl.when(z < 3)
+    def _():
+        onward(-1, z).wait_recv()
+        product[z] = product[z] + left_in[z].astype(jnp.float32)
+
+    own = pl.ds(pl.multiple_of(z * rows, rows), rows)
+    tokens = jnp.concatenate([pieces[i, own, :] for i in range(4)], 1).astype(jnp.float32)
+    after = (tokens + product[z].astype(jnp.bfloat16).astype(jnp.float32)).astype(jnp.bfloat16)
+    after_ref[...] = after
+    after = after.astype(jnp.float32)
+    mean = jnp.mean(after * after, axis=1, keepdims=True)
+    rows_ref[:, :width] = (
+        after * lax.rsqrt(mean + 1e-05) * gain_ref[1:2, :].astype(jnp.float32)
+    ).astype(jnp.bfloat16)
+    rows_ref[:, width:] = tail_ref[...]
+    for way in (1, -1):
+        for s in range(3):
+
+            @pl.when(can_send(way, s))
+            def _(way=way, s=s):
+                hop(way, s).wait_send()
+
+        for d in (1, 2, 3) if way > 0 else (0, 1, 2):
+
+            @pl.when(passing(way, d))
+            def _(way=way, d=d):
+                onward(way, d).wait_send()
+
+
+def attend(length, hidden, norm_gain, qk_gain, cosine, sine, tail, w_qkv, cache, w_out):
+    span, cols = hidden.shape
+    width = cols * 4
+    rows = span // 4
+    half = jnp.bfloat16
+    vmem = pl.BlockSpec(memory_space=pltpu.VMEM)
+    anywhere = pl.BlockSpec(memory_space=pl.ANY)
+    dma = pltpu.SemaphoreType.DMA
+    return pl.pallas_call(
+        attend_kernel,
+        out_shape=(
+            jax.ShapeDtypeStruct((rows, width + TAIL), half),
+            jax.ShapeDtypeStruct((rows, width), half),
+            jax.ShapeDtypeStruct((2, span, cols), half),
+        ),
+        in_specs=[pl.BlockSpec(memory_space=pltpu.SMEM)] + [vmem] * 6 + [anywhere] * 3,
+        out_specs=(vmem, vmem, vmem),
+        scratch_shapes=[
+            pltpu.VMEM((4, span, cols), half),
+            pltpu.VMEM(w_qkv.shape, half),
+            pltpu.VMEM(cache.shape, half),
+            pltpu.VMEM(w_out.shape, half),
+            pltpu.VMEM((3, span, cols), jnp.float32),
+            pltpu.VMEM((span, 128), jnp.float32),
+            pltpu.VMEM((span, cols), half),
+            pltpu.VMEM((4, rows, width), jnp.float32),
+            pltpu.VMEM((4, rows, width), half),
+            pltpu.VMEM((4, rows, width), half),
+            pltpu.VMEM((4, rows, width), half),
+            pltpu.VMEM((4, rows, width), half),
+            dma((3,)),
+            dma((2, 3)),
+            dma((2, 3)),
+            pltpu.VMEM((8, span), jnp.float32),
+            dma((4,)),
+            pltpu.VMEM((4, 8, span), jnp.float32),
+            dma((4,)),
+            dma((2, 4)),
+            dma((2, 4)),
+        ],
+        compiler_params=pltpu.CompilerParams(
+            collective_id=2, has_side_effects=True, vmem_limit_bytes=VMEM_LIMIT
+        ),
+        name="attend",
+    )(length, hidden, norm_gain, qk_gain, cosine, sine, tail, w_qkv, cache, w_out)
+
+
+def layer_by_copies(
+    hidden, norm_gain, w_qkv, qk_gain, w_out, cache, lengths, placing, routes, gate_w, w_gu, w_down
+):
+    position = lax.axis_index("wide")
+    column = lax.axis_index("narrow")
+    span = hidden.shape[1]
+    rows, width = span // 4, hidden.shape[2] * 4
     held, _, _, inner = w_gu.shape
-    experts = held * 8
-    column = lax.axis_index("narrow")
-    routed = normalize(after_rows, gain).astype(jnp.bfloat16)
+    length = jnp.sum(
+        jnp.where(jnp.arange(lengths.shape[0], dtype=jnp.int32) == placing[position], lengths, 0)
+    )
+    positions = length.astype(jnp.float32) + jnp.arange(span, dtype=jnp.float32)
+    frequency = 10000.0 ** (-(jnp.arange(HD // 2, dtype=jnp.float32) * (2.0 / HD)))
+    angle = positions[:, None] * frequency[None, :]
+    cosine, sine = jnp.cos(angle), jnp.sin(angle)
     table = router_table(
-        lax.dynamic_slice_in_dim(routes, column * rows, rows, 0),
-        lax.dynamic_slice_in_dim(gate_w, column * rows, rows, 0),
-        experts,
-    )
-    filler = jnp.zeros((rows, TAIL - 3 * experts), jnp.bfloat16)
-    rows_in = jnp.concatenate([routed] + in_three(table) + [filler], 1)
+        lax.dynamic_slice_in_dim(routes[0], column * rows, rows, 0),
+        lax.dynamic_slice_in_dim(gate_w[0], column * rows, rows, 0),
+        held * 8,
+    )
+    filler = jnp.zeros((rows, TAIL - 24 * held), jnp.bfloat16)
+    rows_in, after_rows, fresh = attend(
+        length.reshape(1),
+        hidden[0],
+        norm_gain,
+        qk_gain,
+        jnp.concatenate([cosine, cosine], 1),
+        jnp.concatenate([-sine, sine], 1),
+        jnp.concatenate(in_three(table) + [filler], 1),
+        jnp.transpose(w_qkv, (1, 0, 2)),
+        cache[:, 0],
+        w_out,
+    )
     weighted = gather_experts(rows_in, w_gu.reshape(held, width, 2 * inner))
-    return reduce_experts(weighted, w_down.reshape(held * inner, width), after_rows)
+    result = reduce_experts(weighted, w_down.reshape(held * inner, width), after_rows)
+    return result[None], fresh[:, None]
 
 
 def experts_by_collectives(after_rows, gain, routes, gate_w, w_gu, w_down):
@@ -405,7 +729,6 @@
     hidden, norm_gain, w_qkv, qk_gain, w_out, cache, lengths, placing, routes, gate_w, w_gu, w_down
 ):
     narrow = lax.axis_size("narrow")
-    wide_size = lax.axis_size("wide")
     column = lax.axis_index("narrow")
     position = lax.axis_index("wide")
     span_len = hidden.shape[1]
@@ -457,9 +780,9 @@
     ).astype(jnp.float32)
     own_rows = lax.dynamic_slice_in_dim(tokens, column * rows, rows, 0)
     after_rows = (own_rows.astype(jnp.float32) + attention).astype(jnp.bfloat16)
-    by_copies = wide_size == 8 and narrow == 4 and w_gu.shape[0] * 24 <= TAIL
-    experts_of = experts_by_copies if by_copies else experts_by_collectives
-    result = experts_of(after_rows, norm_gain[1], routes[0], gate_w[0], w_gu, w_down)[None]
+    result = experts_by_collectives(
+        after_rows, norm_gain[1], routes[0], gate_w[0], w_gu, w_down
+    )[None]
     fresh = jnp.stack(
         [keys_new.reshape(span_len, local_cols), values_new.reshape(span_len, local_cols)]
     )[:, None]
@@ -481,8 +804,9 @@
         P("wide", None, None, "narrow"),
         P("wide", "narrow", None),
     )
+    by_copies = mesh.shape["wide"] == 8 and mesh.shape["narrow"] == 4
     return jax.shard_map(
-        per_device,
+        layer_by_copies if by_copies else per_device,
         mesh=mesh,
         in_specs=placed,
         out_specs=(P("wide", None, "narrow"), P(None, "wide", None, "narrow")),

time: 226 us -> 189 us (0.84)
  Pallas kernels: 105 us -> 171 us
  local copies, waits for them, and re-layouts: 48.2 us -> 12.4 us
  waiting for transfers between devices: 16.1 us -> 0 us
  between operations: 16.9 us -> 1.36 us
  blocking collectives: 13.4 us -> 0 us
  matrix products: 11.6 us -> 0 us
  other arithmetic: 13.2 us -> 4.07 us
    pallas_call x0 -> x1, Pallas kernels: none -> 66.2 us  [attend(): pl.pallas_call(attend_kernel, out_shape=(jax.ShapeDtypeStruct((rows, widt...]
    reduce_scatter x1 -> x0, waiting for transfers between devices: 15.3 us -> none  [per_device(): lax.psum_scatter(partial_out.astype(jnp.bfloat16), 'narrow', scatter_dime...]
    psum x1 -> x0, blocking collectives: 13.4 us -> none  [per_device(): lax.psum((jnp.sum(queries * queries, -1), jnp.sum(keys_new * keys_new, -1...]
    unnamed x25 -> x6, local copies, waits for them, and re-layouts: 15.6 us -> 2.48 us
    slice x6 -> x0, local copies, waits for them, and re-layouts: 11.8 us -> none  [the longest x2 8.51 us: per_device(): cache[1, 0].reshape(stored, head_count, HD)]
    dot_general x4 -> x0, matrix products: 11.6 us -> none  [the longest x1 4.96 us: per_device(): jnp.dot(normed, w_qkv.reshape(full_width, 3 * local_cols), preferred_elem...]
    another operation x1 -> x0, local copies, waits for them, and re-layouts: 3.97 us -> none  [per_device(): cache[0, 0].reshape(stored, head_count, HD)]
    reduce_sum x4 -> x1, other arithmetic: 5.4 us -> 1.96 us  [layer_by_copies(): jnp.sum(jnp.where(jnp.arange(lengths.shape[0], dtype=jnp.int32) == placin...]
  transfers between devices with their start and end apart: 2 -> 0, of which waited for: 2 -> 0; matrix products, arithmetic and copies ran while one was open for 18% -> 0% of each run, Pallas kernels for 0% -> 0%
where the time goes in v3:
time: 189 us
  Pallas kernels  171 us (90%)
  local copies, waits for them, and re-layouts  12.4 us (7%)
  other arithmetic  4.07 us (2%)
    pallas_call x1, Pallas kernels, attend(): pl.pallas_call(attend_kernel, out_shape=(jax.ShapeDtypeStruct((rows, widt...  66.2 us
    pallas_call x1, Pallas kernels, reduce_experts(): pl.pallas_call(reduce_kernel, out_shape=jax.ShapeDtypeStruct((span, cols)...  56.2 us
    pallas_call x1, Pallas kernels, gather_experts(): pl.pallas_call(gather_kernel, out_shape=jax.ShapeDtypeStruct((4, 8, rows,...  48.3 us
    reshape x1, local copies, waits for them, and re-layouts, layer_by_copies(): weighted = gather_experts(rows_in, w_gu.reshape(held, width, 2 * inner))  7.59 us

profile of v3, /device:TPU:0, one launch (start us, length us, event | category | flops | bytes accessed | tf_op | source)
XLA Modules:
  0.0 188.6 jit_solution(5100471780645165170)
XLA Ops:
  0.6 0.0 copy-start
  0.7 1.2 dynamic_slice.9
  1.9 2.0 %fusion.2 = s32[]{:T(128)} fusion(s32[8]{0:T(128)} %param.18, s32[]{:T(128)} %bitcast), kind=kLoop, calls=%fused_computation.15 | loop fusion | flops 23 | bytes 40 | tf_op jit(solution)/shard_map/reduce_sum | solution.py:659
  4.5 0.1 pad.3.clone
  4.6 0.0 copy-done
  4.6 0.1 dynamic-slice_bitcast_fusion.1
  4.7 0.8 dynamic-slice_bitcast_fusion
  5.5 0.1 copy.23
  5.6 0.1 copy.22
  5.7 0.7 maximum_maximum_fusion.tail_ref
  6.4 0.5 fusion
  6.9 0.8 pad_maximum_fusion
  7.7 66.2 %attend.1 = (bf16[64,2176]{1,0:T(8,128)(2,1)}, bf16[64,2048]{1,0:T(8,128)(2,1)}, bf16[2,256,512]{2,1,0:T(8,128)(2,1)}) custom-call(s32[1]{0:T(128)} %bitcast.1.length_ref, bf16[256,512]{1,0:T(8,128)(2,1)} %bitcast.19, bf16[2,2048]{1,0:T(2,128)(2,1)} %gain_ref.1, f32[2,512]{1,0:T(2,128)} %qk_gain_ref.1, f32[256,128]{1,0:T(8,128)} %get-tuple-element.21.cosine_ref, ...), custom_call_target="tpu_custom_call" | custom-call | tf_op jit(solution)/shard_map/attend/pallas_call | solution.py:612
  74.0 7.6 %reshape.30.gu_ref = bf16[2,2048,512]{2,1,0:T(8,128)(2,1)} reshape(bf16[2,2048,2,256]{3,2,1,0:T(2,128)(2,1)} %param.22) | data formatting | bytes 8388608 | tf_op jit(solution)/shard_map/reshape | solution.py:684
  81.5 48.3 %gather_experts.1.weighted_ref = bf16[4,8,64,512]{3,2,1,0:T(8,128)(2,1)} custom-call(bf16[64,2176]{1,0:T(8,128)(2,1)} %get-tuple-element.5.rows_ref, bf16[2,2048,512]{2,1,0:T(8,128)(2,1)} %reshape.30.gu_ref), custom_call_target="tpu_custom_call" | custom-call | tf_op jit(solution)/shard_map/gather_experts/pallas_call | solution.py:175
  129.9 0.0 copy-start.1
  129.9 56.2 %reduce_experts.1 = bf16[256,512]{1,0:T(8,128)(2,1)} custom-call(bf16[4,8,64,512]{3,2,1,0:T(8,128)(2,1)} %gather_experts.1.weighted_ref, bf16[512,2048]{1,0:T(8,128)(2,1)} %bitcast.16, bf16[64,2048]{1,0:T(8,128)(2,1)} %get-tuple-element.6.after_ref), custom_call_target="tpu_custom_call" | custom-call | tf_op jit(solution)/shard_map/reduce_experts/pallas_call | solution.py:307
  186.1 1.7 copy.27
  187.8 0.0 copy-done.1
  187.8 0.8 copy.28
  (6 shorter events, 0.1 us)
Async XLA Ops:
  0.6 4.0 %copy-start = (s32[1,256,8]{1,2,0:T(8,128)S(1)}, s32[1,256,8]{1,2,0:T(8,128)}, u32[]{:S(2)}) copy-start(s32[1,256,8]{1,2,0:T(8,128)} %param.20) | copy-start | bytes 24580
  129.9 57.9 %copy-start.1 = (bf16[2,256,512]{2,1,0:T(8,128)(2,1)S(1)}, bf16[2,256,512]{2,1,0:T(8,128)(2,1)}, u32[]{:S(2)}) copy-start(bf16[2,256,512]{2,1,0:T(8,128)(2,1)} %get-tuple-element.7) | copy-start | bytes 1572868

commit v4 on v3

--- a/solution.py
+++ b/solution.py
@@ -35,6 +35,7 @@
 
 
 TAIL = 128
+PARTS = 2
 VMEM_LIMIT = 56 * 1024 * 1024
 
 
@@ -65,7 +66,7 @@
     pl.semaphore_wait(barrier, 6)
 
 
-def gather_kernel(rows_ref, gu_ref, out_ref, held, send, recv):
+def gather_kernel(rows_ref, gu_ref, out_ref, held, send, recv, z_send, z_recv):
     w, z, sib, first, second = places()
     width = gu_ref.shape[1]
     inner = gu_ref.shape[2] // 2
@@ -77,9 +78,11 @@
     held[z, w] = rows_ref[...]
     greet(w, z, sib, first, second)
     started = []
+    upper = lax.div(z, 2)
+    order = (z, z + 1 - 2 * lax.rem(z, 2), 2 - upper, 3 - 3 * upper)
 
     def piece(slot, k, role, device):
-        ref = held.at[lax.rem(z + 4 - k, 4), slot]
+        ref = held.at[order[k], slot]
         return pltpu.make_async_remote_copy(
             src_ref=ref,
             dst_ref=ref,
@@ -95,7 +98,7 @@
         started.append(copy)
 
     def arrive(role, k):
-        ref = held.at[lax.rem(z + 4 - k, 4), slots[role]]
+        ref = held.at[order[k], slots[role]]
         pltpu.make_async_remote_copy(
             src_ref=ref,
             dst_ref=ref,
@@ -106,7 +109,7 @@
         ).wait_recv()
 
     def expert_rows(k):
-        group = lax.rem(z + 4 - k, 4)
+        group = order[k]
 
         def half(h, carry):
             rows = held.shape[2]
@@ -128,45 +131,59 @@
 
         lax.fori_loop(0, 2, half, 0)
 
-    for k in (1, 3, 2):
-        ref = held.at[z, w]
-        copy = pltpu.make_async_remote_copy(
+    def along(src, way):
+        ref = held.at[src, w]
+        return pltpu.make_async_remote_copy(
             src_ref=ref,
             dst_ref=ref,
-            send_sem=send.at[len(started)],
-            recv_sem=recv.at[0, k],
-            device_id={"narrow": lax.rem(z + k, 4)},
+            send_sem=z_send.at[(way + 1) // 2, src],
+            recv_sem=z_recv.at[src],
+            device_id={"narrow": lax.rem(z + way + 4, 4)},
             device_id_type=pl.DeviceIdType.MESH,
         )
-        copy.start()
-        started.append(copy)
-    order = (0, 1, 3, 2)
+
+    def sends(src, way):
+        return (src <= z) & (z < 3) if way > 0 else (src >= z) & (z > 0)
+
+    def pass_on(src):
+        for way in (1, -1):
+
+            @pl.when(sends(src, way))
+            def _(way=way):
+                along(src, way).start()
+
+    pass_on(z)
     for t in range(7):
         if t < 4:
-            k = order[t]
-            if k:
-                arrive(0, k)
-            push(w, k, 1, first)
-            push(w, k, 2, second)
-            push(w, k, 4, sib)
+            push(w, t, 1, first)
+            push(w, t, 2, second)
+            push(w, t, 4, sib)
+        if t < 3:
+            along(order[t + 1], 1).wait_recv()
+            pass_on(order[t + 1])
         if 1 <= t < 5:
-            k = order[t - 1]
+            k = t - 1
             arrive(1, k)
             push(slots[1], k, 3, second)
             push(slots[1], k, 5, sib)
             arrive(2, k)
             push(slots[2], k, 6, sib)
         if 2 <= t < 6:
-            k = order[t - 2]
+            k = t - 2
             arrive(3, k)
             push(slots[3], k, 7, sib)
         if 3 <= t:
-            k = order[t - 3]
             for role in (4, 5, 6, 7):
-                arrive(role, k)
-            expert_rows(k)
+                arrive(role, t - 3)
+            expert_rows(t - 3)
     for copy in started:
         copy.wait_send()
+    for src in order:
+        for way in (1, -1):
+
+            @pl.when(sends(src, way))
+            def _(src=src, way=way):
+                along(src, way).wait_send()
 
 
 def gather_experts(rows_in, gu):
@@ -179,8 +196,10 @@
         out_specs=pl.BlockSpec(memory_space=pltpu.VMEM),
         scratch_shapes=[
             pltpu.VMEM((4, 8, rows, padded), jnp.bfloat16),
-            pltpu.SemaphoreType.DMA((31,)),
+            pltpu.SemaphoreType.DMA((28,)),
             pltpu.SemaphoreType.DMA((8, 4)),
+            pltpu.SemaphoreType.DMA((2, 4)),
+            pltpu.SemaphoreType.DMA((4,)),
         ],
         compiler_params=pltpu.CompilerParams(
             collective_id=0, has_side_effects=True, vmem_limit_bytes=VMEM_LIMIT
@@ -239,59 +258,67 @@
             device_id_type=pl.DeviceIdType.MESH,
         ).wait_recv()
 
+    share = cols // PARTS
+
     def columns(k):
         return pl.ds(pl.multiple_of(lax.rem(z + k, 4) * cols, cols), cols)
 
     def product(slot, k):
+        start = lax.rem(z + k // PARTS, 4) * cols + k % PARTS * share
         values = weighted_ref[:, slot].reshape(span, weighted_ref.shape[3])
-        return jnp.dot(values, down_ref[:, columns(k)], preferred_element_type=jnp.float32)
+        return jnp.dot(
+            values,
+            down_ref[:, pl.ds(pl.multiple_of(start, share), share)],
+            preferred_element_type=jnp.float32,
+        )
 
     for k in (1, 3, 2):
         push(
             after_ref.at[:, columns(k)],
             after_in.at[k],
-            20 + k,
+            16 * PARTS + k,
             {"narrow": lax.rem(z + k, 4)},
         )
-    order = (2, 1, 3, 0)
-    for t in range(7):
-        if t < 4:
+    order = [k * PARTS + p for k in (2, 1, 3, 0) for p in range(PARTS)]
+    count = len(order)
+    for t in range(count + 3):
+        if t < count:
             k = order[t]
             for r in range(4):
                 sib_out[k, r] = product(w + theirs[r], k).astype(jnp.bfloat16)
             push(sib_out.at[k], sib_in.at[k], k, {"wide": w + sib})
-        if 1 <= t < 5:
+        if 1 <= t < count + 1:
             k = order[t - 1]
             arrive(sib_in.at[k], k)
             for spot, r in ((0, 1), (1, 3)):
                 value = product(w + mine[r], k) + sib_in[k, r].astype(jnp.float32)
                 first_out[k, spot] = value.astype(jnp.bfloat16)
-            push(first_out.at[k], first_in.at[k], 4 + k, {"wide": w + first})
+            push(first_out.at[k], first_in.at[k], 4 * PARTS + k, {"wide": w + first})
             for spot, r in ((0, 0), (1, 2)):
                 first_keep[k, spot] = product(w + mine[r], k) + sib_in[k, r].astype(jnp.float32)
-        if 2 <= t < 6:
+        if 2 <= t < count + 2:
             k = order[t - 2]
-            arrive(first_in.at[k], 4 + k)
+            arrive(first_in.at[k], 4 * PARTS + k)
             second_out[k] = (first_keep[k, 1] + first_in[k, 1].astype(jnp.float32)).astype(
                 jnp.bfloat16
             )
-            push(second_out.at[k], second_in.at[k], 8 + k, {"wide": w + second})
+            push(second_out.at[k], second_in.at[k], 8 * PARTS + k, {"wide": w + second})
             second_keep[k] = first_keep[k, 0] + first_in[k, 0].astype(jnp.float32)
         if 3 <= t:
             k = order[t - 3]
-            arrive(second_in.at[k], 8 + k)
+            arrive(second_in.at[k], 8 * PARTS + k)
             value = second_keep[k] + second_in[k].astype(jnp.float32)
-            if k:
+            if k >= PARTS:
                 z_out[k] = value.astype(jnp.bfloat16)
-                push(z_out.at[k], z_in.at[k], 12 + k, {"narrow": lax.rem(z + k, 4)})
+                push(z_out.at[k], z_in.at[k], 12 * PARTS + k, {"narrow": lax.rem(z + k // PARTS, 4)})
             else:
-                total[...] = value
+                total[:, k * share : (k + 1) * share] = value
     for k in (1, 2, 3):
-        arrive(z_in.at[k], 12 + k)
-        arrive(after_in.at[k], 20 + k)
-    total[...] = total[...] + (
-        z_in[1].astype(jnp.float32) + z_in[2].astype(jnp.float32) + z_in[3].astype(jnp.float32)
-    )
+        arrive(after_in.at[k], 16 * PARTS + k)
+    for n in order[: 3 * PARTS]:
+        arrive(z_in.at[n], 12 * PARTS + n)
+        at = slice(n % PARTS * share, (n % PARTS + 1) * share)
+        total[:, at] = total[:, at] + z_in[n].astype(jnp.float32)
     for k in range(4):
         block = pl.ds(pl.multiple_of(lax.rem(z + 4 - k, 4) * rows, rows), rows)
         own = after_in[k] if k else after_ref[:, columns(0)]
@@ -303,6 +330,7 @@
 def reduce_experts(weighted, down, after_rows):
     rows, width = after_rows.shape
     span, cols = rows * 4, width // 4
+    parts, share = 4 * PARTS, cols // PARTS
     half = jnp.bfloat16
     return pl.pallas_call(
         reduce_kernel,
@@ -310,20 +338,20 @@
         in_specs=[pl.BlockSpec(memory_space=pltpu.VMEM)] * 3,
         out_specs=pl.BlockSpec(memory_space=pltpu.VMEM),
         scratch_shapes=[
-            pltpu.VMEM((4, 4, span, cols), half),
-            pltpu.VMEM((4, 4, span, cols), half),
-            pltpu.VMEM((4, 2, span, cols), half),
-            pltpu.VMEM((4, 2, span, cols), jnp.float32),
-            pltpu.VMEM((4, 2, span, cols), half),
-            pltpu.VMEM((4, span, cols), half),
-            pltpu.VMEM((4, span, cols), jnp.float32),
-            pltpu.VMEM((4, span, cols), half),
-            pltpu.VMEM((4, span, cols), half),
-            pltpu.VMEM((4, span, cols), half),
+            pltpu.VMEM((parts, 4, span, share), half),
+            pltpu.VMEM((parts, 4, span, share), half),
+            pltpu.VMEM((parts, 2, span, share), half),
+            pltpu.VMEM((parts, 2, span, share), jnp.float32),
+            pltpu.VMEM((parts, 2, span, share), half),
+            pltpu.VMEM((parts, span, share), half),
+            pltpu.VMEM((parts, span, share), jnp.float32),
+            pltpu.VMEM((parts, span, share), half),
+            pltpu.VMEM((parts, span, share), half),
+            pltpu.VMEM((parts, span, share), half),
             pltpu.VMEM((4, rows, cols), half),
             pltpu.VMEM((span, cols), jnp.float32),
-            pltpu.SemaphoreType.DMA((24,)),
-            pltpu.SemaphoreType.DMA((24,)),
+            pltpu.SemaphoreType.DMA((16 * PARTS + 4,)),
+            pltpu.SemaphoreType.DMA((16 * PARTS + 4,)),
         ],
         compiler_params=pltpu.CompilerParams(
             collective_id=1, has_side_effects=True, vmem_limit_bytes=VMEM_LIMIT

time: 189 us -> 181 us (0.958)
  Pallas kernels: 171 us -> 163 us
    pallas_call x1, Pallas kernels: 56.2 us -> 46.6 us  [reduce_experts(): pl.pallas_call(reduce_kernel, out_shape=jax.ShapeDtypeStruct((span, cols)...]
where the time goes in v4:
time: 181 us
  Pallas kernels  163 us (90%)
  local copies, waits for them, and re-layouts  12.4 us (7%)
  other arithmetic  4.07 us (2%)
    pallas_call x1, Pallas kernels, attend(): pl.pallas_call(attend_kernel, out_shape=(jax.ShapeDtypeStruct((rows, widt...  66.2 us
    pallas_call x1, Pallas kernels, gather_experts(): pl.pallas_call(gather_kernel, out_shape=jax.ShapeDtypeStruct((4, 8, rows,...  50.1 us
    pallas_call x1, Pallas kernels, reduce_experts(): pl.pallas_call(reduce_kernel, out_shape=jax.ShapeDtypeStruct((span, cols)...  46.6 us
    reshape x1, local copies, waits for them, and re-layouts, layer_by_copies(): weighted = gather_experts(rows_in, w_gu.reshape(held, width, 2 * inner))  7.59 us

profile of v4, /device:TPU:0, one launch (start us, length us, event | category | flops | bytes accessed | tf_op | source)
XLA Modules:
  0.0 180.8 jit_solution(2628193113386005293)
XLA Ops:
  0.6 0.0 copy-start
  0.7 1.2 dynamic_slice.9
  1.9 2.0 %fusion.2 = s32[]{:T(128)} fusion(s32[8]{0:T(128)} %param.18, s32[]{:T(128)} %bitcast), kind=kLoop, calls=%fused_computation.15 | loop fusion | flops 23 | bytes 40 | tf_op jit(solution)/shard_map/reduce_sum | solution.py:687
  4.5 0.1 pad.3.clone
  4.6 0.0 copy-done
  4.6 0.1 dynamic-slice_bitcast_fusion.1
  4.7 0.8 dynamic-slice_bitcast_fusion
  5.5 0.1 copy.23
  5.6 0.1 copy.22
  5.7 0.7 maximum_maximum_fusion.tail_ref
  6.4 0.5 fusion
  6.9 0.8 pad_maximum_fusion
  7.7 66.2 %attend.1 = (bf16[64,2176]{1,0:T(8,128)(2,1)}, bf16[64,2048]{1,0:T(8,128)(2,1)}, bf16[2,256,512]{2,1,0:T(8,128)(2,1)}) custom-call(s32[1]{0:T(128)} %bitcast.1.length_ref, bf16[256,512]{1,0:T(8,128)(2,1)} %bitcast.19, bf16[2,2048]{1,0:T(2,128)(2,1)} %gain_ref.1, f32[2,512]{1,0:T(2,128)} %qk_gain_ref.1, f32[256,128]{1,0:T(8,128)} %get-tuple-element.21.cosine_ref, ...), custom_call_target="tpu_custom_call" | custom-call | tf_op jit(solution)/shard_map/attend/pallas_call | solution.py:640
  74.0 7.6 %reshape.30.gu_ref = bf16[2,2048,512]{2,1,0:T(8,128)(2,1)} reshape(bf16[2,2048,2,256]{3,2,1,0:T(2,128)(2,1)} %param.22) | data formatting | bytes 8388608 | tf_op jit(solution)/shard_map/reshape | solution.py:712
  81.5 50.1 %gather_experts.1.weighted_ref = bf16[4,8,64,512]{3,2,1,0:T(8,128)(2,1)} custom-call(bf16[64,2176]{1,0:T(8,128)(2,1)} %get-tuple-element.5.rows_ref, bf16[2,2048,512]{2,1,0:T(8,128)(2,1)} %reshape.30.gu_ref), custom_call_target="tpu_custom_call" | custom-call | tf_op jit(solution)/shard_map/gather_experts/pallas_call | solution.py:192
  131.7 0.0 copy-start.1
  131.7 46.6 %reduce_experts.1 = bf16[256,512]{1,0:T(8,128)(2,1)} custom-call(bf16[4,8,64,512]{3,2,1,0:T(8,128)(2,1)} %gather_experts.1.weighted_ref, bf16[512,2048]{1,0:T(8,128)(2,1)} %bitcast.16, bf16[64,2048]{1,0:T(8,128)(2,1)} %get-tuple-element.6.after_ref), custom_call_target="tpu_custom_call" | custom-call | tf_op jit(solution)/shard_map/reduce_experts/pallas_call | solution.py:335
  178.3 1.7 copy.27
  180.0 0.0 copy-done.1
  180.0 0.8 copy.28
  (6 shorter events, 0.1 us)
Async XLA Ops:
  0.6 4.0 %copy-start = (s32[1,256,8]{1,2,0:T(8,128)S(1)}, s32[1,256,8]{1,2,0:T(8,128)}, u32[]{:S(2)}) copy-start(s32[1,256,8]{1,2,0:T(8,128)} %param.20) | copy-start | bytes 24580
  131.7 48.3 %copy-start.1 = (bf16[2,256,512]{2,1,0:T(8,128)(2,1)S(1)}, bf16[2,256,512]{2,1,0:T(8,128)(2,1)}, u32[]{:S(2)}) copy-start(bf16[2,256,512]{2,1,0:T(8,128)(2,1)} %get-tuple-element.7) | copy-start | bytes 1572868
